TPU v7x, 512 devices: a whole 4x4x16 slice. The times are simulated.
512 devices in a mesh: row: 8 (over x, y_lo), col: 16 (over z), rep: 4 (over y_hi, core).
Axes of the slice: x: 4, y: 4 (y_hi: 2, y_lo: 2; y = y_hi * 2 + y_lo), z: 16, core: 2. Of those that a mesh axis runs over, the one named last changes fastest.
Arguments:
- features: float32 [262144, 256], P(('row', 'col', 'rep')), may hold values from -6 to 6
- self_weight: float32 [256, 256], replicated, may hold values from -0.375 to 0.375
- neigh_weight: float32 [256, 256], replicated, may hold values from -1.2 to 1.2
- block_source: int32 [4096, 8], P(('row', 'col', 'rep')), may hold values from 0 to 95, as said below
- edge_weights: int32 [4096, 8, 64, 64], P(('row', 'col', 'rep')), may hold values from 0 to 15, as said below
- labels: int32 [262144], P(('row', 'col', 'rep')), may hold values from 0 to 255
Outputs:
- grad_self: float32 [256, 256], replicated
- grad_neigh: float32 [256, 256], replicated
- grad_features: float32 [262144, 256], P(('row', 'col', 'rep'))
Inputs may be any that keep to these rules, and one draw needn't show every extreme that they name: `block_source`: slot 0 of every block row names the row's own block. `edge_weights`: in each block row the filled slots come first, with entries 1 to 15; later slots are all zero. Every block row has 1 to 8 filled slots, and some block row has all 8.
All inputs are finite; a program needn't handle non-finite values.
Results may differ from a plain program's by a relative error of at most 0.0035.
Values may be sent and summed in bfloat16 or wider, within the bound.
A program may use at most 64 MiB of HBM per device.

v0:
```python
import jax
import jax.numpy as jnp
from jax import lax
from jax.sharding import PartitionSpec as P

BLOCK = 64


def extended(value, sides, width):
    for axis, dim in sides:
        devices, length = (lax.axis_size(axis), value.shape[dim])
        up = [(i, (i + 1) % devices) for i in range(devices)]
        down = [(j, i) for i, j in up]
        last = lax.slice_in_dim(value, length - width, length, axis=dim)
        first = lax.slice_in_dim(value, 0, width, axis=dim)
        before = lax.ppermute(last, axis, up)
        after = lax.ppermute(first, axis, down)
        value = jnp.concatenate([before, value, after], axis=dim)
    return value


def on_device(features, self_weight, neigh_weight, block_source, edge_weights, labels):
    high = lax.Precision.HIGHEST
    row_count, width_in = features.shape
    block_count = row_count // BLOCK
    lowered = features.astype(jnp.bfloat16)
    gathered_group = lax.all_gather(lowered, "rep", axis=0, tiled=True)
    neighbours = extended(gathered_group[None], (("col", 0),), 1)
    group_blocks = neighbours.shape[1] // BLOCK
    table = neighbours.reshape(3 * group_blocks, BLOCK, width_in)
    source_peer = block_source // group_blocks
    inner_block = block_source % group_blocks
    table_index = jnp.where(
        source_peer == 0,
        group_blocks + inner_block,
        jnp.where(source_peer == 1, inner_block, block_source),
    )
    weights_low = edge_weights.astype(jnp.bfloat16)
    degree = jnp.sum(edge_weights, axis=(1, 3)).astype(jnp.float32)[..., None]
    aggregated = jnp.einsum(
        "bsij,bsjf->bif", weights_low, table[table_index], preferred_element_type=jnp.float32
    )
    neighbour_mean = (aggregated / degree).reshape(row_count, width_in)
    logits = jnp.dot(features, self_weight, precision=high) + jnp.dot(
        neighbour_mean, neigh_weight, precision=high
    )
    class_total = self_weight.shape[1]
    target = (labels[:, None] == jnp.arange(class_total, dtype=jnp.int32)[None, :]).astype(
        jnp.float32
    )
    residual = jax.nn.sigmoid(logits) - target
    contract_rows = (((0,), (0,)), ((), ()))
    self_part = lax.dot_general(features, residual, contract_rows, precision=high)
    neigh_part = lax.dot_general(neighbour_mean, residual, contract_rows, precision=high)
    grad_self, grad_neigh = lax.psum((self_part, neigh_part), ("row", "col", "rep"))
    spread = (
        jnp.dot(residual, neigh_weight.T, precision=high).reshape(block_count, BLOCK, width_in)
        / degree
    ).astype(jnp.bfloat16)
    empty_terms = jnp.zeros((3 * group_blocks, BLOCK, width_in), jnp.float32)
    contrib = jnp.einsum("bsij,bif->bsjf", weights_low, spread, preferred_element_type=jnp.float32)
    partial_sum = empty_terms.at[table_index.reshape(-1)].add(contrib.reshape(-1, BLOCK, width_in))
    terms = partial_sum.astype(jnp.bfloat16).reshape(3, group_blocks * BLOCK, width_in)
    outgoing = terms[0::2]
    incoming = extended(outgoing, (("col", 0),), 1)
    region_terms = (
        terms[1].astype(jnp.float32)
        + incoming[0].astype(jnp.float32)
        + incoming[3].astype(jnp.float32)
    )
    own_terms = lax.psum_scatter(region_terms, "rep", scatter_dimension=0, tiled=True)
    grad_features = jnp.dot(residual, self_weight.T, precision=high) + own_terms
    return (grad_self, grad_neigh, grad_features)


def solution(mesh):
    return jax.shard_map(
        on_device,
        mesh=mesh,
        in_specs=(
            P(("row", "col", "rep"), None),
            P(),
            P(),
            P(("row", "col", "rep"), None),
            P(("row", "col", "rep"), None, None, None),
            P(("row", "col", "rep")),
        ),
        out_specs=(P(), P(), P(("row", "col", "rep"), None)),
        check_vma=False,
    )
```

profile of v0, /device:TPU:1, one launch (start us, length us, event | category | flops | bytes accessed | tf_op | source)
XLA Modules:
  0.0 647.4 jit_solution(5769744073268807981)
XLA Ops:
  7.2 0.0 copy-start
  7.2 0.0 copy-start.1
  7.2 0.0 copy-start.5
  7.2 0.0 all-gather.2.cloned.1.call-start
  7.2 1.8 convert_element_type.40
  9.1 0.0 all-gather.2.cloned.1.call-update
  9.1 0.0 all-reduce.3.cloned.1.call-start
  9.2 35.7 %all-gather.2.cloned.1.call-done = bf16[2048,256]{1,0:T(8,128)(2,1)} async-done(((bf16[512,256]{1,0:T(8,128)(2,1)}), bf16[2048,256]{1,0:T(8,128)(2,1)}) %all-gather.2.cloned.1.call-update) | async-done | bytes 1048592 | tf_op jit(solution)/shard_map/all_gather | solution.py:27
  44.8 5.7 collective-permute-start.1
  50.5 1.9 collective-permute-start
  52.4 0.7 compare_select_fusion
  53.1 0.1 reshape.75
  53.2 0.1 reshape.66
  53.3 2.6 fusion.11
  56.0 1.3 copy.9
  57.3 1.4 fusion.12
  58.7 14.3 %collective-permute-done.1 = bf16[1,2048,256]{2,1,0:T(8,128)(2,1)S(1)} collective-permute-done((bf16[1,2048,256]{2,1,0:T(8,128)(2,1)}, bf16[1,2048,256]{2,1,0:T(8,128)(2,1)S(1)}, u32[]{:S(2)}, u32[]{:S(2)}) %collective-permute-start.1) | collective-permute-done | bytes 1048608 | tf_op jit(solution)/shard_map/ppermute | solution.py:17
  73.0 1.0 copy-done.7
  74.0 4.1 collective-permute-done
  78.1 2.2 pad_maximum_fusion
  80.3 2.0 gather_fusion
  82.3 2.5 fusion.5
  84.8 0.7 fusion.4
  85.5 0.6 fusion.15
  86.1 2.8 fusion.6
  88.9 3.4 broadcast_in_dim.15
  92.3 13.6 %scatter_fusion = f32[96,64,256]{2,1,0:T(8,128)} fusion(f32[96,64,256]{2,1,0:T(8,128)} %broadcast_in_dim.15, s32[64]{0:T(128)S(1)} %fusion.9, f32[64,64,256]{2,1,0:T(8,128)} %bitcast.49), kind=kCustom, calls=%fused_computation.1 | custom fusion | flops 1048576 | bytes 12583168 | tf_op jit(solution)/shard_map/scatter-add | solution.py:62
  105.9 3.3 convert_element_type.45
  109.2 0.1 slice.14
  109.3 0.0 copy-start.2
  109.3 1.5 fusion.10
  110.8 1.9 collective-permute-start.2
  112.7 4.6 collective-permute-start.3
  117.3 0.1 slice.19
  117.4 1.7 fusion.13
  119.1 1.7 convolution_bitcast_fusion.1
  120.8 0.0 all-reduce.3.cloned.1.call-update
  120.8 0.0 reduce-scatter.2.cloned.1.call-start
  120.9 16.3 %collective-permute-done.2 = bf16[1,2048,256]{2,1,0:T(8,128)(2,1)S(1)} collective-permute-done((bf16[1,2048,256]{2,1,0:T(8,128)(2,1)}, bf16[1,2048,256]{2,1,0:T(8,128)(2,1)S(1)}, u32[]{:S(2)}, u32[]{:S(2)}) %collective-permute-start.2) | collective-permute-done | bytes 1048608 | tf_op jit(solution)/shard_map/ppermute | solution.py:16
  137.2 1.1 collective-permute-done.3
  138.3 2.9 convert_add_fusion
  141.2 0.0 reduce-scatter.2.cloned.1.call-update
  141.2 0.6 fusion.14
  141.9 442.1 %all-reduce.3.cloned.1.call-done = (f32[256,256]{0,1:T(8,128)}, f32[256,256]{1,0:T(8,128)}) async-done(((f32[256,256]{0,1:T(8,128)}, f32[256,256]{1,0:T(8,128)}), (f32[256,256]{0,1:T(8,128)}, f32[256,256]{1,0:T(8,128)})) %all-reduce.3.cloned.1.call-update) | async-done | bytes 524304 | tf_op jit(solution)/shard_map/psum | solution.py:55
  584.0 1.8 copy.10
  585.8 51.5 %reduce-scatter.2.cloned.1.call-done = f32[512,256]{1,0:T(8,128)} async-done(((f32[2048,256]{1,0:T(8,128)}), f32[512,256]{1,0:T(8,128)}) %reduce-scatter.2.cloned.1.call-update) | async-done | bytes 524304 | tf_op jit(solution)/shard_map/reduce_scatter | solution.py:71
  637.3 1.9 add.63
  639.2 1.7 copy.15
  (18 shorter events, 0.0 us)
Async XLA Ops:
  7.2 77.6 %copy-start = (f32[256,256]{1,0:T(8,128)S(1)}, f32[256,256]{1,0:T(8,128)}, u32[]{:S(2)}) copy-start(f32[256,256]{1,0:T(8,128)} %param.8) | copy-start | bytes 786436
  7.2 50.1 %copy-start.1 = (f32[512,256]{1,0:T(8,128)S(1)}, f32[512,256]{1,0:T(8,128)}, u32[]{:S(2)}) copy-start(f32[512,256]{1,0:T(8,128)} %param.6) | copy-start | bytes 1572868
  7.2 50.1 %copy-start.5 = (f32[256,256]{1,0:T(8,128)S(1)}, f32[256,256]{1,0:T(8,128)}, u32[]{:S(2)}) copy-start(f32[256,256]{1,0:T(8,128)} %param.7) | copy-start | bytes 786436
  7.2 37.6 %all-gather.2.cloned.1.call-start = ((), (), s32[]{:S(2)}) async-start(), calls=%async_computation.1 | async-start | bytes 1310720 | tf_op jit(solution)/shard_map/all_gather | solution.py:27
  9.1 574.9 %all-reduce.3.cloned.1.call-start = ((), (), s32[]{:S(2)}) async-start(), calls=%async_computation.3 | async-start | bytes 1048576 | tf_op jit(solution)/shard_map/psum | solution.py:55
  44.8 28.2 %collective-permute-start.1 = (bf16[1,2048,256]{2,1,0:T(8,128)(2,1)}, bf16[1,2048,256]{2,1,0:T(8,128)(2,1)S(1)}, u32[]{:S(2)}, u32[]{:S(2)}) collective-permute-start(bf16[1,2048,256]{2,1,0:T(8,128)(2,1)} %bitcast.55), channel_id=1, source_target_pairs={{4,0},{8,4},{12,8},{16,12},{20,16},{24,20},{28,24},{32,28},{36,32}... | collective-permute-start | bytes 3145736 | tf_op jit(solution)/shard_map/ppermute | solution.py:17
  50.5 27.6 %collective-permute-start = (bf16[1,2048,256]{2,1,0:T(8,128)(2,1)}, bf16[1,2048,256]{2,1,0:T(8,128)(2,1)}, u32[]{:S(2)}, u32[]{:S(2)}) collective-permute-start(bf16[1,2048,256]{2,1,0:T(8,128)(2,1)} %bitcast.56), channel_id=1, source_target_pairs={{0,4},{4,8},{8,12},{12,16},{16,20},{20,24},{24,28},{28,32},{32,36}... | collective-permute-start | bytes 3145736 | tf_op jit(solution)/shard_map/ppermute | solution.py:16
  56.0 17.1 %copy-start.4 = (bf16[8,8,64,64]{3,2,1,0:T(8,128)(2,1)}, bf16[8,8,64,64]{3,2,1,0:T(8,128)(2,1)S(1)}, u32[]{:S(2)}) copy-start(bf16[8,8,64,64]{3,2,1,0:T(8,128)(2,1)S(1)} %get-tuple-element.13) | copy-start | bytes 1572868
  73.0 1.0 copy-start.7
  82.3 2.5 copy-start.8
  82.3 2.5 copy-start.9
  84.8 1.3 copy-start.3
  109.3 9.8 %copy-start.2 = (f32[512,256]{1,0:T(8,128)S(1)}, f32[512,256]{1,0:T(8,128)}, u32[]{:S(2)}) copy-start(f32[512,256]{1,0:T(8,128)} %param.6) | copy-start | bytes 1572868
  110.8 26.4 %collective-permute-start.2 = (bf16[1,2048,256]{2,1,0:T(8,128)(2,1)}, bf16[1,2048,256]{2,1,0:T(8,128)(2,1)S(1)}, u32[]{:S(2)}, u32[]{:S(2)}) collective-permute-start(bf16[1,2048,256]{2,1,0:T(8,128)(2,1)} %get-tuple-element.10), channel_id=1, source_target_pairs={{0,4},{4,8},{8,12},{12,16},{16,20},{20,24},{24,28},{28,32},{32,36}... | collective-permute-start | bytes 3145736 | tf_op jit(solution)/shard_map/ppermute | solution.py:16
  112.7 25.6 %collective-permute-start.3 = (bf16[1,2048,256]{2,1,0:T(8,128)(2,1)}, bf16[1,2048,256]{2,1,0:T(8,128)(2,1)}, u32[]{:S(2)}, u32[]{:S(2)}) collective-permute-start(bf16[1,2048,256]{2,1,0:T(8,128)(2,1)} %get-tuple-element.11), channel_id=1, source_target_pairs={{4,0},{8,4},{12,8},{16,12},{20,16},{24,20},{28,24},{32,28},{36,32}... | collective-permute-start | bytes 3145736 | tf_op jit(solution)/shard_map/ppermute | solution.py:17
  120.8 20.4 %copy-start.6 = (f32[256,256]{1,0:T(8,128)S(1)}, f32[256,256]{1,0:T(8,128)}, u32[]{:S(2)}) copy-start(f32[256,256]{1,0:T(8,128)} %param.7) | copy-start | bytes 786436
  120.8 516.5 %reduce-scatter.2.cloned.1.call-start = ((), (), s32[]{:S(2)}) async-start(), calls=%async_computation.2 | async-start | bytes 2621440 | tf_op jit(solution)/shard_map/reduce_scatter | solution.py:71
Sparse Core Ops, SparseCore 0:
  10.7 34.1 all-gather.1
  120.9 463.0 all-reduce.2
  587.1 50.1 reduce-scatter.1
where the time goes:
time: 648 us; the launch traced here: 647 us
  waiting for transfers between devices  565 us (87%)
  other arithmetic  29 us (4%)
  starting transfers between devices  14.2 us (2%)
  between operations  14 us (2%)
  local copies, waits for them, and re-layouts  13.1 us (2%)
  matrix products  11.9 us (2%)
    psum x1, waiting for transfers between devices, on_device(): lax.psum((self_part, neigh_part), ('row', 'col', 'rep'))  442 us
    reduce_scatter x1, waiting for transfers between devices, on_device(): lax.psum_scatter(region_terms, 'rep', scatter_dimension=0, tiled=True)  51.5 us
    all_gather x1, waiting for transfers between devices, on_device(): gathered_group = lax.all_gather(lowered, 'rep', axis=0, tiled=True)  35.7 us
    ppermute x2, waiting for transfers between devices, extended(): before = lax.ppermute(last, axis, up)  20.4 us
    ppermute x2, waiting for transfers between devices, extended(): after = lax.ppermute(first, axis, down)  15.4 us
    scatter-add x1, other arithmetic, on_device(): empty_terms.at[table_index.reshape(-1)]  13.6 us
  transfers between devices with their start and end apart: 7, of which 7 were waited for; matrix products, arithmetic and copies ran while one was open for 2% of the time, Pallas kernels for 0%

commit v1 on v0

v1 whole, which is shorter than its diff:
```python
import functools

import jax
import jax.numpy as jnp
from jax import lax
from jax.experimental import pallas as pl
from jax.experimental.pallas import tpu as pltpu
from jax.sharding import PartitionSpec as P

MESH = pl.DeviceIdType.MESH
BF = jnp.bfloat16
F32 = jnp.float32
BLOCK = 64
ROWS = 512
NK = 4
CH = ROWS // NK
ORDER = (0, 2, 1, 3)
HIGH = lax.Precision.HIGHEST
DMA = pltpu.SemaphoreType.DMA
VM = pl.BlockSpec(memory_space=pltpu.VMEM)
SM = pl.BlockSpec(memory_space=pltpu.SMEM)


def remote(src, dst, ssem, rsem, dev):
    return pltpu.make_async_remote_copy(
        src_ref=src, dst_ref=dst, send_sem=ssem, recv_sem=rsem, device_id=dev, device_id_type=MESH
    )


class Place:
    def __init__(self, nx, nz):
        self.nx, self.nz = nx, nz
        row, self.z, self.rep = lax.axis_index("row"), lax.axis_index("col"), lax.axis_index("rep")
        self.x, self.ylo = row // 2, row % 2
        self.yhi, self.core = self.rep // 2, self.rep % 2
        self.y = self.yhi * 2 + self.ylo
        self.row = row

    def at(self, x, y, z, core):
        return {"row": x * 2 + y % 2, "col": z, "rep": (y // 2) * 2 + core}

    def partner(self):
        return self.at(self.x, self.y, self.z, 1 - self.core)

    def ystep(self, d):
        return self.at(self.x, (self.y + d) % 4, self.z, self.core)

    def zto(self, z):
        return self.at(self.x, self.y, z, self.core)

    def zstep(self, d):
        return self.zto((self.z + d) % self.nz)


def signal(devs):
    barrier = pltpu.get_barrier_semaphore()
    for dev in devs:
        pl.semaphore_signal(barrier, inc=1, device_id=dev, device_id_type=MESH)
    return barrier


def rows(k):
    return pl.ds(k * CH, CH)


def gather_kernel(nx, nz, f_ref, t_ref, relay, ps, pr, zs, zr, ys, yr, rs, rr):
    me = Place(nx, nz)
    partner = me.partner()
    up, down = me.zstep(1), me.zstep(nz - 1)
    yup, ydown = me.ystep(1), me.ystep(3)
    barrier = signal((partner, up, down, yup, ydown))
    rep = me.rep
    other = (1 - me.yhi) * 2 + me.core
    t_ref[rep] = f_ref[...].astype(BF)
    pl.semaphore_wait(barrier, 5)

    started = []

    def go(copy):
        copy.start()
        started.append(copy)

    def slot(m, mine, across):
        return (mine, across, 4 + mine, 8 + mine, 4 + across, 8 + across)[m]

    def to_partner(m, k):
        ref = t_ref.at[slot(m, rep, other), rows(k)]
        go(remote(ref, ref, ps.at[m, k], pr.at[m, k], partner))

    def from_partner(m, k):
        prep, pother = me.yhi * 2 + 1 - me.core, (1 - me.yhi) * 2 + 1 - me.core
        ref = t_ref.at[slot(m, prep, pother), rows(k)]
        remote(ref, ref, ps.at[m, k], pr.at[m, k], partner).wait_recv()

    def to_z(half, k):
        mine = (rep, other)[half]
        src = t_ref.at[mine, rows(k)]
        go(remote(src, t_ref.at[4 + mine, rows(k)], zs.at[0, half, k], zr.at[0, half, k], up))
        go(remote(src, t_ref.at[8 + mine, rows(k)], zs.at[1, half, k], zr.at[1, half, k], down))

    def z_arrived(half, k):
        mine = (rep, other)[half]
        for d in (0, 1):
            ref = t_ref.at[4 + 4 * d + mine, rows(k)]
            remote(ref, ref, zs.at[d, half, k], zr.at[d, half, k], up).wait_recv()
            to_partner(2 + 2 * half + d, k)

    def ydev(k):
        return yup if k < 2 else ydown

    def to_relay(k):
        go(remote(t_ref.at[rep, rows(k)], relay.at[rows(k)], ys.at[k], rr.at[k], ydev(k)))

    def relay_on(k):
        ref = relay.at[rows(k)]
        remote(ref, ref, ys.at[k], rr.at[k], yup).wait_recv()
        origin = (me.y + (3 if k < 2 else 1)) % 4
        dst = t_ref.at[(origin // 2) * 2 + me.core, rows(k)]
        go(remote(ref, dst, rs.at[k], yr.at[k], ydev(k)))

    def y_arrived(k):
        ref = t_ref.at[other, rows(k)]
        remote(ref, ref, rs.at[k], yr.at[k], yup).wait_recv()
        to_z(1, k)
        to_partner(1, k)

    for k in ORDER:
        to_relay(k)
        to_z(0, k)
    for k in ORDER:
        to_partner(0, k)
    relay_on(0)
    relay_on(2)
    z_arrived(0, 0)
    relay_on(1)
    relay_on(3)
    z_arrived(0, 2)
    y_arrived(0)
    y_arrived(2)
    z_arrived(0, 1)
    y_arrived(1)
    y_arrived(3)
    z_arrived(0, 3)
    for k in ORDER:
        z_arrived(1, k)
    for m in range(6):
        for k in ORDER:
            from_partner(m, k)
    for copy in started:
        copy.wait_send()


def gather(nx, nz, features):
    return pl.pallas_call(
        functools.partial(gather_kernel, nx, nz),
        out_shape=jax.ShapeDtypeStruct((12, ROWS, 256), BF),
        in_specs=[VM],
        out_specs=VM,
        scratch_shapes=[
            pltpu.VMEM((ROWS, 256), BF),
            DMA((6, NK)),
            DMA((6, NK)),
            DMA((2, 2, NK)),
            DMA((2, 2, NK)),
            DMA((NK,)),
            DMA((NK,)),
            DMA((NK,)),
            DMA((NK,)),
        ],
        compiler_params=pltpu.CompilerParams(collective_id=0, has_side_effects=True),
        name="gather_tables",
    )(features)


def dot(a, b, dims=((1,), (0,)), precision=None):
    return lax.dot_general(
        a, b, (dims, ((), ())), precision=precision, preferred_element_type=F32
    )


def local_kernel(
    src, fill, t_ref, f_ref, ws_ref, wn_ref, ew_ref, lab_ref, terms_ref, grads_ref, own_ref, acc, mean, deg, touched
):
    wide = []
    ones = jnp.ones((8 * BLOCK, 256), BF)
    for b in range(8):
        cat = jnp.concatenate([ew_ref[b, s].astype(F32).astype(BF) for s in range(8)], axis=1)
        wide.append(cat)
        table = jnp.concatenate([t_ref[src[b, s]] for s in range(8)], axis=0)
        d = dot(cat, ones)
        here = pl.ds(b * BLOCK, BLOCK)
        deg[here, :] = d
        mean[here, :] = dot(cat, table) / d
    feats, m = f_ref[...], mean[...]
    logits = dot(feats, ws_ref[...], precision=HIGH) + dot(m, wn_ref[...], precision=HIGH)
    label = jnp.broadcast_to(lab_ref[...].astype(F32), (256, ROWS)).T
    column = lax.broadcasted_iota(jnp.int32, (ROWS, 256), 1).astype(F32)
    residual = 1.0 / (1.0 + jnp.exp(-logits)) - jnp.where(label == column, 1.0, 0.0)
    turn = ((0,), (0,))
    last = ((1,), (1,))
    for i, left in enumerate((feats, m)):
        part = dot(left, residual, turn, precision=HIGH)
        for h in (0, 1):
            grads_ref[h, i * 256 : (i + 1) * 256, :] = part[:, h * 128 : (h + 1) * 128]
    own_ref[...] = dot(residual, ws_ref[...], last, precision=HIGH)
    spread = (dot(residual, wn_ref[...], last, precision=HIGH) / deg[...]).astype(BF)

    @pl.loop(0, 96)
    def _(t):
        touched[t] = 0

    for b in range(8):
        flipped = wide[b].astype(F32).T.astype(BF)
        contrib = dot(flipped, spread[b * BLOCK : (b + 1) * BLOCK, :])
        for s in range(8):
            mine = contrib[s * BLOCK : (s + 1) * BLOCK, :]
            t = src[b, s]

            @pl.when(fill[b, s] > 0)
            def _():
                @pl.when(touched[t] == 0)
                def _():
                    acc[t] = mine

                @pl.when(touched[t] > 0)
                def _():
                    acc[t] += mine

                touched[t] = 1

    @pl.loop(0, 96)
    def _(t):
        @pl.when(touched[t] > 0)
        def _():
            terms_ref[t] = acc[t].astype(BF)

        @pl.when(touched[t] == 0)
        def _():
            terms_ref[t] = jnp.zeros((BLOCK, 256), BF)


def local(table, features, self_weight, neigh_weight, block_source, edge_weights, labels):
    fill = (edge_weights[:, :, 0, 0] > 0).astype(jnp.int32)
    return pl.pallas_call(
        local_kernel,
        out_shape=(
            jax.ShapeDtypeStruct((96, BLOCK, 256), BF),
            jax.ShapeDtypeStruct((2, ROWS, 128), F32),
            jax.ShapeDtypeStruct((ROWS, 256), F32),
        ),
        in_specs=[SM, SM] + [VM] * 6,
        out_specs=(VM, VM, VM),
        scratch_shapes=[
            pltpu.VMEM((96, BLOCK, 256), F32),
            pltpu.VMEM((ROWS, 256), F32),
            pltpu.VMEM((ROWS, 256), F32),
            pltpu.SMEM((96,), jnp.int32),
        ],
        compiler_params=pltpu.CompilerParams(vmem_limit_bytes=48 << 20),
        name="local_math",
    )(
        block_source,
        fill,
        table.reshape(96, BLOCK, 256),
        features,
        self_weight,
        neigh_weight,
        edge_weights,
        labels.reshape(1, ROWS),
    )


def reduce_kernel(
    nx, nz, tm_ref, g_ref, own_ref, gs_ref, gn_ref, out_ref,
    pair, zsend, zgot, ysend, relay, ygot, gpair, total, plane, quad, far, part, full,
    ps, pr, zs, zr, ys, yr, rs, rr, gps, gpr, pls, plr, qs, qr, fs, fr, aqs, aqr, aps, apr, gfs, gfr,
):
    me = Place(nx, nz)
    partner = me.partner()
    core, yhi, z = me.core, me.yhi, me.z
    up, down = me.zstep(1), me.zstep(nz - 1)
    yup, ydown = me.ystep(1), me.ystep(3)
    flat = me.x * 4 + me.y
    q, h = z % 4, z // 4
    far_n = nz // 4
    planes = nx * 4

    def plane_dev(p):
        return me.at(p // 4, p % 4, z, core)

    barrier = signal((partner, up, down))

    @pl.loop(1, planes)
    def _(d):
        pl.semaphore_signal(barrier, inc=1, device_id=plane_dev((flat + d) % planes), device_id_type=MESH)

    for d in range(1, 4):
        pl.semaphore_signal(barrier, inc=1, device_id=me.zto(h * 4 + (q + d) % 4), device_id_type=MESH)
    for d in range(1, far_n):
        pl.semaphore_signal(barrier, inc=1, device_id=me.zto((h + d) % far_n * 4 + q), device_id_type=MESH)
    pl.semaphore_wait(barrier, 3 + planes - 1 + 3 + far_n - 1)

    started = []

    def go(copy):
        copy.start()
        started.append(copy)

    halves = (1 - yhi, yhi)

    go(remote(g_ref.at[1 - core], gpair, gps.at[0], gpr.at[0], partner))

    def pair_out(reg, half, k):
        yh = halves[half]
        go(
            remote(
                tm_ref.at[reg * 4 + yh * 2 + 1 - core, rows(k)],
                pair.at[reg * 2 + half, rows(k)],
                ps.at[reg * 2 + half, k],
                pr.at[reg * 2 + half, k],
                partner,
            )
        )

    def pair_sum(reg, half, k):
        ref = pair.at[reg * 2 + half, rows(k)]
        remote(ref, ref, ps.at[reg * 2 + half, k], pr.at[reg * 2 + half, k], partner).wait_recv()
        mine = tm_ref[reg * 4 + halves[half] * 2 + core, rows(k), :]
        return mine.astype(F32) + pair[reg * 2 + half, rows(k), :].astype(F32)

    def z_out(half, k):
        for d in (0, 1):
            zsend[d * 2 + half, rows(k), :] = pair_sum(1 + d, half, k).astype(BF)
            go(
                remote(
                    zsend.at[d * 2 + half, rows(k)],
                    zgot.at[d * 2 + half, rows(k)],
                    zs.at[d * 2 + half, k],
                    zr.at[d * 2 + half, k],
                    (down, up)[d],
                )
            )

    def region_sum(half, k):
        value = pair_sum(0, half, k)
        for d in (0, 1):
            ref = zgot.at[d * 2 + half, rows(k)]
            remote(ref, ref, zs.at[d * 2 + half, k], zr.at[d * 2 + half, k], up).wait_recv()
            value = value + zgot[d * 2 + half, rows(k), :].astype(F32)
        return value

    def ydev(k):
        return yup if k < 2 else ydown

    def y_out(k):
        ysend[rows(k), :] = region_sum(0, k).astype(BF)
        go(remote(ysend.at[rows(k)], relay.at[rows(k)], ys.at[k], rr.at[k], ydev(k)))

    def relay_on(k):
        ref = relay.at[rows(k)]
        remote(ref, ref, ys.at[k], rr.at[k], yup).wait_recv()
        go(remote(ref, ygot.at[rows(k)], rs.at[k], yr.at[k], ydev(k)))

    def finish(k):
        value = region_sum(1, k) + own_ref[rows(k), :]
        ref = ygot.at[rows(k)]
        remote(ref, ref, rs.at[k], yr.at[k], yup).wait_recv()
        out_ref[rows(k), :] = value + ygot[rows(k), :].astype(F32)

    for k in ORDER:
        pair_out(1, 0, k)
        pair_out(2, 0, k)
    for k in ORDER:
        pair_out(0, 0, k)
    for k in ORDER:
        pair_out(1, 1, k)
        pair_out(2, 1, k)
    for k in ORDER:
        pair_out(0, 1, k)

    remote(gpair, gpair, gps.at[0], gpr.at[0], partner).wait_recv()
    total[...] = g_ref[core] + gpair[...]
    width = ROWS // planes

    def piece(p):
        return pl.ds(pl.multiple_of(p * width, width), width)

    def plane_copy(d):
        p = (flat + d) % planes
        return remote(total.at[piece(p)], plane.at[flat], pls.at[d], plr.at[d], plane_dev(p))

    @pl.loop(1, planes)
    def _(d):
        plane_copy(d).start()

    for k in ORDER:
        z_out(0, k)

    plane[flat] = total[piece(flat), :]

    @pl.loop(1, planes)
    def _(d):
        ref = plane.at[(flat + planes - d) % planes]
        remote(ref, ref, pls.at[d], plr.at[d], partner).wait_recv()

    summed = plane[0]
    for p in range(1, planes):
        summed = summed + plane[p]
    part[...] = summed.reshape(4, width // 4, 128)
    quad[q] = part[q]

    def quad_copy(d):
        other = (q + d) % 4
        return remote(part.at[other], quad.at[q], qs.at[d], qr.at[d], me.zto(h * 4 + other))

    for d in range(1, 4):
        quad_copy(d).start()
    z_out(1, 0)
    z_out(1, 2)
    for d in range(1, 4):
        ref = quad.at[(q + 4 - d) % 4]
        remote(ref, ref, qs.at[d], qr.at[d], partner).wait_recv()
    far[h] = quad[0] + quad[1] + quad[2] + quad[3]

    def far_copy(d):
        return remote(far.at[h], far.at[h], fs.at[d], fr.at[d], me.zto((h + d) % far_n * 4 + q))

    for d in range(1, far_n):
        far_copy(d).start()
    z_out(1, 1)
    z_out(1, 3)
    y_out(0)
    y_out(2)
    y_out(1)
    y_out(3)
    for d in range(1, far_n):
        ref = far.at[(h + far_n - d) % far_n]
        remote(ref, ref, fs.at[d], fr.at[d], partner).wait_recv()
    for d in range(1, 4):
        quad_copy(d).wait_send()
    summed = far[0]
    for j in range(1, far_n):
        summed = summed + far[j]
    mine = full.at[core, piece(flat)]
    tile = width // 4

    def inner(j):
        return full.at[core, pl.ds(pl.multiple_of(flat * width + j * tile, tile), tile)]

    full[core, pl.ds(pl.multiple_of(flat * width + q * tile, tile), tile), :] = summed

    def again_copy(d):
        return remote(inner(q), inner(q), aqs.at[d], aqr.at[d], me.zto(h * 4 + (q + d) % 4))

    for d in range(1, 4):
        again_copy(d).start()
    for k in ORDER:
        relay_on(k)
    for d in range(1, 4):
        ref = inner((q + 4 - d) % 4)
        remote(ref, ref, aqs.at[d], aqr.at[d], partner).wait_recv()

    def spread_copy(d):
        return remote(mine, mine, aps.at[d], apr.at[d], plane_dev((flat + d) % planes))

    @pl.loop(1, planes)
    def _(d):
        spread_copy(d).start()

    for k in ORDER:
        finish(k)

    @pl.loop(1, planes)
    def _(d):
        ref = full.at[core, piece((flat + planes - d) % planes)]
        remote(ref, ref, aps.at[d], apr.at[d], partner).wait_recv()

    last = remote(full.at[core], full.at[core], gfs.at[0], gfr.at[0], partner)
    last.start()
    remote(full.at[1 - core], full.at[1 - core], gfs.at[0], gfr.at[0], partner).wait_recv()
    for i, ref in enumerate((gs_ref, gn_ref)):
        for c in (0, 1):
            ref[:, c * 128 : (c + 1) * 128] = full[c, i * 256 : (i + 1) * 256, :]

    last.wait_send()
    for d in range(1, 4):
        again_copy(d).wait_send()
    for d in range(1, far_n):
        far_copy(d).wait_send()

    @pl.loop(1, planes)
    def _(d):
        plane_copy(d).wait_send()
        spread_copy(d).wait_send()

    for copy in started:
        copy.wait_send()


def reduce_all(nx, nz, terms, grads, own):
    planes, far_n = nx * 4, nz // 4
    width = ROWS // planes
    big = (6, NK)
    return pl.pallas_call(
        functools.partial(reduce_kernel, nx, nz),
        out_shape=(
            jax.ShapeDtypeStruct((256, 256), F32),
            jax.ShapeDtypeStruct((256, 256), F32),
            jax.ShapeDtypeStruct((ROWS, 256), F32),
        ),
        in_specs=[VM] * 3,
        out_specs=(VM,) * 3,
        scratch_shapes=[
            pltpu.VMEM((6, ROWS, 256), BF),
            pltpu.VMEM((4, ROWS, 256), BF),
            pltpu.VMEM((4, ROWS, 256), BF),
            pltpu.VMEM((ROWS, 256), BF),
            pltpu.VMEM((ROWS, 256), BF),
            pltpu.VMEM((ROWS, 256), BF),
            pltpu.VMEM((ROWS, 128), F32),
            pltpu.VMEM((ROWS, 128), F32),
            pltpu.VMEM((planes, width, 128), F32),
            pltpu.VMEM((4, width // 4, 128), F32),
            pltpu.VMEM((far_n, width // 4, 128), F32),
            pltpu.VMEM((4, width // 4, 128), F32),
            pltpu.VMEM((2, ROWS, 128), F32),
            DMA(big), DMA(big), DMA((4, NK)), DMA((4, NK)),
            DMA((NK,)), DMA((NK,)), DMA((NK,)), DMA((NK,)),
            DMA((1,)), DMA((1,)), DMA((planes,)), DMA((planes,)),
            DMA((4,)), DMA((4,)), DMA((far_n,)), DMA((far_n,)),
            DMA((4,)), DMA((4,)), DMA((planes,)), DMA((planes,)),
            DMA((1,)), DMA((1,)),
        ],
        compiler_params=pltpu.CompilerParams(
            collective_id=1, has_side_effects=True, vmem_limit_bytes=48 << 20
        ),
        name="reduce_all",
    )(terms.reshape(12, ROWS, 256), grads, own)


def solution(mesh):
    nx, nz = mesh.shape["row"] // 2, mesh.shape["col"]
    split = P(("row", "col", "rep"))

    def on_device(features, self_weight, neigh_weight, block_source, edge_weights, labels):
        table = gather(nx, nz, features)
        terms, grads, own = local(
            table, features, self_weight, neigh_weight, block_source, edge_weights, labels
        )
        return reduce_all(nx, nz, terms, grads, own)

    return jax.shard_map(
        on_device,
        mesh=mesh,
        in_specs=(split, P(), P(), split, split, split),
        out_specs=(P(), P(), split),
        check_vma=False,
    )
```

time: 648 us -> 90.8 us (0.14)
  waiting for transfers between devices: 565 us -> 0 us
  Pallas kernels: 0 us -> 84.4 us
  other arithmetic: 29 us -> 0.01 us
  starting transfers between devices: 14.2 us -> 0 us
  between operations: 14 us -> 0.75 us
  matrix products: 11.9 us -> 0 us
  local copies, waits for them, and re-layouts: 13.1 us -> 5.35 us
    psum x1 -> x0, waiting for transfers between devices: 442 us -> none  [on_device(): lax.psum((self_part, neigh_part), ('row', 'col', 'rep'))]
    pallas_call x0 -> x3, Pallas kernels: none -> 84.4 us  [the longest x1 38.2 us: reduce_all(): pl.pallas_call(functools.partial(reduce_kernel, nx, nz), out_shape=(jax.S...]
    reduce_scatter x1 -> x0, waiting for transfers between devices: 51.5 us -> none  [on_device(): lax.psum_scatter(region_terms, 'rep', scatter_dimension=0, tiled=True)]
    ppermute x4 -> x0, waiting for transfers between devices: 35.8 us -> none  [the longest x2 20.4 us: extended(): before = lax.ppermute(last, axis, up)]
    all_gather x1 -> x0, waiting for transfers between devices: 35.7 us -> none  [on_device(): gathered_group = lax.all_gather(lowered, 'rep', axis=0, tiled=True)]
    ppermute x4 -> x0, starting transfers between devices: 14.1 us -> none  [the longest x2 10.2 us: extended(): after = lax.ppermute(first, axis, down)]
    scatter-add x1 -> x0, other arithmetic: 13.6 us -> none  [on_device(): empty_terms.at[table_index.reshape(-1)]]
    dot_general x7 -> x0, matrix products: 9.15 us -> none  [the longest x1 2.46 us: on_device(): jnp.einsum('bsij,bsjf->bif', weights_low, table[table_index], preferred_e...]
  transfers between devices with their start and end apart: 7 -> 0, of which waited for: 7 -> 0; matrix products, arithmetic and copies ran while one was open for 2% -> 0% of each run, Pallas kernels for 0% -> 0%
where the time goes in v1:
time: 90.8 us; the launch traced here: 90.5 us
  Pallas kernels  84.4 us (93%)
  local copies, waits for them, and re-layouts  5.35 us (6%)
    pallas_call x1, Pallas kernels, reduce_all(): pl.pallas_call(functools.partial(reduce_kernel, nx, nz), out_shape=(jax.S...  38.2 us
    pallas_call x1, Pallas kernels, gather(): pl.pallas_call(functools.partial(gather_kernel, nx, nz), out_shape=jax.Sh...  30.8 us
    pallas_call x1, Pallas kernels, local(): pl.pallas_call(local_kernel, out_shape=(jax.ShapeDtypeStruct((96, BLOCK,...  15.4 us
    unnamed x18, local copies, waits for them, and re-layouts  4.23 us

profile of v1, /device:TPU:1, one launch (start us, length us, event | category | flops | bytes accessed | tf_op | source)
XLA Modules:
  0.0 90.5 jit_solution(12943235369722106543)
XLA Ops:
  0.6 0.0 copy-start.1
  0.6 0.0 copy-start.2
  0.7 0.0 copy-start.6
  0.7 0.0 copy-start.5
  0.7 0.0 copy-start.4
  0.7 0.0 copy-start.3
  0.7 1.1 %slice.3 = s32[8,8,1,1]{3,2,1,0:T(1,128)S(1)} slice(s32[8,8,64,64]{3,2,1,0:T(8,128)} %ew_ref.1), slice={[0:8], [0:8], [0:1], [0:1]} | slice | bytes 512 | tf_op jit(solution)/shard_map/slice | solution.py:243
  1.8 0.1 copy.10
  1.9 30.8 %gather_tables.1 = bf16[12,512,256]{2,1,0:T(8,128)(2,1)} custom-call(f32[512,256]{1,0:T(8,128)} %f_ref.3), custom_call_target="tpu_custom_call" | custom-call | tf_op jit(solution)/shard_map/gather_tables/pallas_call | solution.py:154
  32.7 0.0 copy-done.1
  32.7 0.0 copy-done.2
  32.8 0.0 copy-done.6
  32.8 0.0 copy-done.5
  32.8 0.0 copy-done.4
  32.8 0.0 copy-done.3
  32.8 15.4 %local_math.1 = (bf16[96,64,256]{2,1,0:T(8,128)(2,1)}, f32[2,512,128]{2,1,0:T(8,128)S(1)}, f32[512,256]{1,0:T(8,128)S(1)}) custom-call(s32[8,8]{1,0:T(8,128)S(1)} %copy-done.5, s32[8,8]{1,0:T(8,128)S(1)} %convert_bitcast_fusion.fill, bf16[96,64,256]{2,1,0:T(8,128)(2,1)} %bitcast.7, f32[512,256]{1,0:T(8,128)S(1)} %copy-done.2, f32[256,256]{1,0:T(8,128)S(1)} %copy-done.3, ...), custom_call_target="tpu_custom_call" | custom-call | tf_op jit(solution)/shard_map/local_math/pallas_call | solution.py:244
  48.2 0.0 copy-start
  48.2 1.9 %copy-done = bf16[96,64,256]{2,1,0:T(8,128)(2,1)S(1)} copy-done((bf16[96,64,256]{2,1,0:T(8,128)(2,1)S(1)}, bf16[96,64,256]{2,1,0:T(8,128)(2,1)}, u32[]{:S(2)}) %copy-start) | copy-done | bytes 3145752
  50.1 38.2 %reduce_all.1 = (f32[256,256]{1,0:T(8,128)S(1)}, f32[256,256]{1,0:T(8,128)S(1)}, f32[512,256]{1,0:T(8,128)S(1)}) custom-call(bf16[12,512,256]{2,1,0:T(8,128)(2,1)S(1)} %bitcast.5, f32[2,512,128]{2,1,0:T(8,128)S(1)} %get-tuple-element.7.g_ref, f32[512,256]{1,0:T(8,128)S(1)} %get-tuple-element.8.own_ref), custom_call_target="tpu_custom_call" | custom-call | tf_op jit(solution)/shard_map/reduce_all/pallas_call | solution.py:504
  88.3 0.7 copy.14
  89.0 0.7 copy.15
  89.7 0.8 copy.16
  (1 shorter events, 0.0 us)
Async XLA Ops:
  0.6 32.1 %copy-start.1 = (s32[8,8,64,64]{3,2,1,0:T(8,128)S(1)}, s32[8,8,64,64]{3,2,1,0:T(8,128)}, u32[]{:S(2)}) copy-start(s32[8,8,64,64]{3,2,1,0:T(8,128)} %ew_ref.1) | copy-start | bytes 3145732
  0.6 32.1 %copy-start.2 = (f32[512,256]{1,0:T(8,128)S(1)}, f32[512,256]{1,0:T(8,128)}, u32[]{:S(2)}) copy-start(f32[512,256]{1,0:T(8,128)} %f_ref.3) | copy-start | bytes 1572868
  0.7 32.1 %copy-start.6 = (s32[512]{0:T(512)S(1)}, s32[512]{0:T(512)}, u32[]{:S(2)}) copy-start(s32[512]{0:T(512)} %param.11) | copy-start | bytes 6148
  0.7 32.1 %copy-start.5 = (s32[8,8]{1,0:T(8,128)S(1)}, s32[8,8]{1,0:T(8,128)}, u32[]{:S(2)}) copy-start(s32[8,8]{1,0:T(8,128)} %src.1) | copy-start | bytes 772
  0.7 32.1 %copy-start.4 = (f32[256,256]{1,0:T(8,128)S(1)}, f32[256,256]{1,0:T(8,128)}, u32[]{:S(2)}) copy-start(f32[256,256]{1,0:T(8,128)} %wn_ref.1) | copy-start | bytes 786436
  0.7 32.1 %copy-start.3 = (f32[256,256]{1,0:T(8,128)S(1)}, f32[256,256]{1,0:T(8,128)}, u32[]{:S(2)}) copy-start(f32[256,256]{1,0:T(8,128)} %ws_ref.1) | copy-start | bytes 786436
  48.2 1.9 %copy-start = (bf16[96,64,256]{2,1,0:T(8,128)(2,1)S(1)}, bf16[96,64,256]{2,1,0:T(8,128)(2,1)}, u32[]{:S(2)}) copy-start(bf16[96,64,256]{2,1,0:T(8,128)(2,1)} %get-tuple-element.6) | copy-start | bytes 9437188

commit v2 on v1

v2 whole, which is shorter than its diff:
```python
import functools

import jax
import jax.numpy as jnp
from jax import lax
from jax.experimental import pallas as pl
from jax.experimental.pallas import tpu as pltpu
from jax.sharding import PartitionSpec as P

MESH = pl.DeviceIdType.MESH
BF = jnp.bfloat16
F32 = jnp.float32
BLOCK = 64
ROWS = 512
NK = 4
CH = ROWS // NK
ORDER = (0, 2, 1, 3)
DMA = pltpu.SemaphoreType.DMA
VM = pl.BlockSpec(memory_space=pltpu.VMEM)
SM = pl.BlockSpec(memory_space=pltpu.SMEM)


def remote(src, dst, ssem, rsem, dev):
    return pltpu.make_async_remote_copy(
        src_ref=src, dst_ref=dst, send_sem=ssem, recv_sem=rsem, device_id=dev, device_id_type=MESH
    )


class Place:
    def __init__(self, nx, nz):
        self.nx, self.nz = nx, nz
        row, self.z, self.rep = lax.axis_index("row"), lax.axis_index("col"), lax.axis_index("rep")
        self.x, self.ylo = row // 2, row % 2
        self.yhi, self.core = self.rep // 2, self.rep % 2
        self.y = self.yhi * 2 + self.ylo
        self.row = row

    def at(self, x, y, z, core):
        return {"row": x * 2 + y % 2, "col": z, "rep": (y // 2) * 2 + core}

    def partner(self):
        return self.at(self.x, self.y, self.z, 1 - self.core)

    def ystep(self, d):
        return self.at(self.x, (self.y + d) % 4, self.z, self.core)

    def zto(self, z):
        return self.at(self.x, self.y, z, self.core)

    def zstep(self, d):
        return self.zto((self.z + d) % self.nz)


def signal(devs):
    barrier = pltpu.get_barrier_semaphore()
    for dev in devs:
        pl.semaphore_signal(barrier, inc=1, device_id=dev, device_id_type=MESH)
    return barrier


def rows(k):
    return pl.ds(k * CH, CH)


def split(value):
    high = value.astype(BF)
    return high, (value - high.astype(F32)).astype(BF)


def dot(a, b, dims=((1,), (0,))):
    return lax.dot_general(a, b, (dims, ((), ())), preferred_element_type=F32)


def dot3(a, b, dims=((1,), (0,))):
    return dot(a[0], b[0], dims) + (dot(a[0], b[1], dims) + dot(a[1], b[0], dims))


TURN = ((0,), (0,))
LAST = ((1,), (1,))


def sorted_slots(src, sel_ref):
    keys = src.astype(F32)
    grid = jnp.concatenate(
        [jnp.broadcast_to(keys[b : b + 1, :], (8, 8)) for b in range(8)]
        + [jnp.full((64, 8), 96.0, F32)],
        axis=0,
    )
    pick = lax.broadcasted_iota(jnp.int32, (128, 8), 0) % 8 == lax.broadcasted_iota(jnp.int32, (128, 8), 1)
    col = jnp.broadcast_to(jnp.sum(jnp.where(pick, grid, 0.0), axis=1, keepdims=True), (128, 128))
    row_id = lax.broadcasted_iota(jnp.int32, (128, 128), 0).astype(F32)
    lane_id = lax.broadcasted_iota(jnp.int32, (128, 128), 1).astype(F32)
    unique = col * 128.0 + row_id
    rank = jnp.sum(jnp.where(unique.T < unique, 1.0, 0.0), axis=1, keepdims=True)
    place = jnp.where(rank == lane_id, 1.0, 0.0)
    perm = jnp.sum(place * row_id, axis=0, keepdims=True)
    key = jnp.sum(place * col, axis=0, keepdims=True)
    again = jnp.where((key == pltpu.roll(key, 1, 1)) & (lane_id[0:1, :] > 0.0), 1.0, 0.0)
    final = jnp.maximum(jnp.sum(jnp.where(col <= lane_id, 1.0, 0.0), axis=0, keepdims=True) - 1.0, 0.0)
    named = jnp.minimum(jnp.sum(jnp.where(col == lane_id, 1.0, 0.0), axis=0, keepdims=True), 1.0)
    sel_ref[...] = jnp.zeros((8, 128), jnp.int32)
    for i, value in enumerate((perm, again, final, named)):
        sel_ref[i : i + 1, :] = value.astype(jnp.int32)


def gather_kernel(
    nx, nz, f_hbm, ws_hbm, wn_hbm, src_hbm, ew_hbm, lab_hbm,
    t_ref, wide_ref, flip_ref, inv_ref, base_ref, hot_ref, ft_ref, w_ref, sel_ref,
    relay, f_ref, ws_ref, wn_ref, ew_ref, src_ref, lab_ref, ls, ps, pr, zs, zr, ys, yr, rs, rr,
):
    me = Place(nx, nz)
    partner = me.partner()
    up, down = me.zstep(1), me.zstep(nz - 1)
    yup, ydown = me.ystep(1), me.ystep(3)
    barrier = signal((partner, up, down, yup, ydown))
    loads = [
        pltpu.make_async_copy(a, b, ls.at[i])
        for i, (a, b) in enumerate(
            (
                (f_hbm, f_ref),
                (src_hbm, src_ref),
                (ew_hbm, ew_ref),
                (ws_hbm, ws_ref),
                (wn_hbm, wn_ref),
                (lab_hbm, lab_ref),
            )
        )
    ]
    for load in loads:
        load.start()
    rep = me.rep
    other = (1 - me.yhi) * 2 + me.core
    loads[0].wait()
    t_ref[rep] = f_ref[...].astype(BF)
    pl.semaphore_wait(barrier, 5)

    started = []

    def go(copy):
        copy.start()
        started.append(copy)

    def slot(m, mine, across):
        return (mine, across, 4 + mine, 8 + mine, 4 + across, 8 + across)[m]

    def to_partner(m, k):
        ref = t_ref.at[slot(m, rep, other), rows(k)]
        go(remote(ref, ref, ps.at[m, k], pr.at[m, k], partner))

    def from_partner(m, k):
        prep, pother = me.yhi * 2 + 1 - me.core, (1 - me.yhi) * 2 + 1 - me.core
        ref = t_ref.at[slot(m, prep, pother), rows(k)]
        remote(ref, ref, ps.at[m, k], pr.at[m, k], partner).wait_recv()

    def to_z(half, k):
        mine = (rep, other)[half]
        src = t_ref.at[mine, rows(k)]
        go(remote(src, t_ref.at[4 + mine, rows(k)], zs.at[0, half, k], zr.at[0, half, k], up))
        go(remote(src, t_ref.at[8 + mine, rows(k)], zs.at[1, half, k], zr.at[1, half, k], down))

    def z_arrived(half, k):
        mine = (rep, other)[half]
        for d in (0, 1):
            ref = t_ref.at[4 + 4 * d + mine, rows(k)]
            remote(ref, ref, zs.at[d, half, k], zr.at[d, half, k], up).wait_recv()
            to_partner(2 + 2 * half + d, k)

    def ydev(k):
        return yup if k < 2 else ydown

    def to_relay(k):
        go(remote(t_ref.at[rep, rows(k)], relay.at[rows(k)], ys.at[k], rr.at[k], ydev(k)))

    def relay_on(k):
        ref = relay.at[rows(k)]
        remote(ref, ref, ys.at[k], rr.at[k], yup).wait_recv()
        origin = (me.y + (3 if k < 2 else 1)) % 4
        dst = t_ref.at[(origin // 2) * 2 + me.core, rows(k)]
        go(remote(ref, dst, rs.at[k], yr.at[k], ydev(k)))

    def y_arrived(k):
        ref = t_ref.at[other, rows(k)]
        remote(ref, ref, rs.at[k], yr.at[k], yup).wait_recv()
        to_z(1, k)
        to_partner(1, k)

    def widen(first):
        ones = jnp.ones((8 * BLOCK, 256), BF)
        for b in range(first, first + 4):
            here = slice(b * BLOCK, (b + 1) * BLOCK)
            cat = jnp.concatenate([ew_ref[b, s].astype(F32) for s in range(8)], axis=1)
            flip_ref[b * 8 : b * 8 + 8] = cat.T.astype(BF).reshape(8, BLOCK, BLOCK)
            low = cat.astype(BF)
            wide_ref[here, :] = low
            inv_ref[here, :] = 1.0 / dot(low, ones)

    def own_logits():
        for i, ref in enumerate((wn_ref, ws_ref)):
            w_ref[2 * i], w_ref[2 * i + 1] = split(ref[...])
        base_ref[...] = dot3(split(f_ref[...]), (w_ref[2], w_ref[3]))

    def turned():
        ft_ref[0], ft_ref[1] = split(f_ref[...].T)

    def targets():
        label = jnp.broadcast_to(lab_ref[...].astype(F32), (256, ROWS)).T
        column = lax.broadcasted_iota(jnp.int32, (ROWS, 256), 1).astype(F32)
        hot_ref[...] = jnp.where(label == column, 1.0, 0.0)

    for k in ORDER:
        to_relay(k)
        to_z(0, k)
    for k in ORDER:
        to_partner(0, k)
    for load in loads[1:]:
        load.wait()
    sorted_slots(src_ref[...], sel_ref)
    relay_on(0)
    relay_on(2)
    widen(0)
    relay_on(1)
    relay_on(3)
    z_arrived(0, 0)
    z_arrived(0, 2)
    widen(4)
    y_arrived(0)
    y_arrived(2)
    z_arrived(0, 1)
    turned()
    y_arrived(1)
    y_arrived(3)
    own_logits()
    z_arrived(0, 3)
    targets()
    for k in ORDER:
        z_arrived(1, k)
    for m in range(6):
        for k in ORDER:
            from_partner(m, k)
    for copy in started:
        copy.wait_send()


def gather(nx, nz, features, self_weight, neigh_weight, block_source, edge_weights, labels):
    hbm = pl.BlockSpec(memory_space=pltpu.HBM)
    wide = jax.ShapeDtypeStruct((ROWS, 256), F32)
    return pl.pallas_call(
        functools.partial(gather_kernel, nx, nz),
        out_shape=(
            jax.ShapeDtypeStruct((12, ROWS, 256), BF),
            jax.ShapeDtypeStruct((ROWS, ROWS), BF),
            jax.ShapeDtypeStruct((64, BLOCK, BLOCK), BF),
            wide,
            wide,
            wide,
            jax.ShapeDtypeStruct((2, 256, ROWS), BF),
            jax.ShapeDtypeStruct((4, 256, 256), BF),
            jax.ShapeDtypeStruct((8, 128), jnp.int32),
        ),
        in_specs=[hbm] * 6,
        out_specs=(VM,) * 9,
        scratch_shapes=[
            pltpu.VMEM((ROWS, 256), BF),
            pltpu.VMEM((ROWS, 256), F32),
            pltpu.VMEM((256, 256), F32),
            pltpu.VMEM((256, 256), F32),
            pltpu.VMEM((8, 8, BLOCK, BLOCK), jnp.int32),
            pltpu.VMEM((8, 8), jnp.int32),
            pltpu.VMEM((1, ROWS), jnp.int32),
            DMA((6,)),
            DMA((6, NK)),
            DMA((6, NK)),
            DMA((2, 2, NK)),
            DMA((2, 2, NK)),
            DMA((NK,)),
            DMA((NK,)),
            DMA((NK,)),
            DMA((NK,)),
        ],
        compiler_params=pltpu.CompilerParams(
            collective_id=0, has_side_effects=True, vmem_limit_bytes=20 << 20
        ),
        name="gather_tables",
    )(
        *(
            pltpu.with_memory_space_constraint(value, pltpu.HBM)
            for value in (
                features, self_weight, neigh_weight, block_source, edge_weights, labels.reshape(1, ROWS)
            )
        )
    )


def main_kernel(
    nx, nz, src, sel, t_ref, wide_ref, flip_ref, inv_ref, base_ref, hot_ref, ft_ref, w_ref,
    gs_ref, gn_ref, out_ref,
    mean, resid, spread, run, done, tmsend, g,
    pair, zsend, zgot, ysend, relay, ygot, gpair, total, plane, two, far, part, full,
    ps, pr, zs, zr, ys, yr, rs, rr, gps, gpr, pls, plr, qs, qr, fs, fr, aqs, aqr, aps, apr, gfs, gfr,
):
    me = Place(nx, nz)
    partner = me.partner()
    core, yhi, z = me.core, me.yhi, me.z
    up, down = me.zstep(1), me.zstep(nz - 1)
    yup, ydown = me.ystep(1), me.ystep(3)
    flat = me.x * 4 + me.y
    q, h = z % 2, z // 2
    far_n = nz // 2
    planes = nx * 4
    beside = me.zto(2 * h + 1 - q)

    def plane_dev(p):
        return me.at(p // 4, p % 4, z, core)

    barrier = signal((partner, up, down))

    def others(body):
        @pl.loop(0, planes)
        def _(p):
            @pl.when(p != flat)
            def _():
                body(p)

    @others
    def _(p):
        pl.semaphore_signal(barrier, inc=1, device_id=plane_dev(p), device_id_type=MESH)

    for d in range(1, far_n):
        pl.semaphore_signal(barrier, inc=1, device_id=me.zto((h + d) % far_n * 2 + q), device_id_type=MESH)

    started = []

    def go(copy):
        copy.start()
        started.append(copy)

    for b in range(8):
        here = pl.ds(b * BLOCK, BLOCK)
        table = jnp.concatenate([t_ref[src[b, s]] for s in range(8)], axis=0)
        m = dot(wide_ref[here, :], table) * inv_ref[here, :]
        mean[0, here, :], mean[1, here, :] = split(m)
    wn, ws = (w_ref[0], w_ref[1]), (w_ref[2], w_ref[3])
    logits = base_ref[...] + dot3((mean[0], mean[1]), wn)
    resid[0], resid[1] = split(1.0 / (1.0 + jnp.exp(-logits)) - hot_ref[...])

    halves = (1 - yhi, yhi)

    def pair_grad(i):
        here = pl.ds(i * 256, 256)
        return remote(g.at[1 - core, here], gpair.at[here], gps.at[i], gpr.at[i], partner)

    def weight_grad(i):
        if i == 0:
            value = dot3((ft_ref[0], ft_ref[1]), (resid[0], resid[1]))
        else:
            value = dot3((mean[0], mean[1]), (resid[0], resid[1]), TURN)
        for c in (0, 1):
            g[c, i * 256 : (i + 1) * 256, :] = value[:, c * 128 : (c + 1) * 128]

    weight_grad(0)
    pl.semaphore_wait(barrier, 3 + planes - 1 + far_n - 1)
    pair_grad(0).start()
    weight_grad(1)
    pair_grad(1).start()

    def block_terms(reg, r, k):
        found = []
        for j in range(CH // BLOCK):
            t = reg * 32 + r * 8 + k * (CH // BLOCK) + j
            found.append(done[sel[2, t]].astype(F32) * sel[3, t].astype(F32))
        return jnp.concatenate(found, axis=0)

    def pair_out(reg, half, k):
        at = reg * 2 + half
        tmsend[at, rows(k), :] = block_terms(reg, halves[half] * 2 + 1 - core, k).astype(BF)
        go(
            remote(
                tmsend.at[at, rows(k)], pair.at[at, rows(k)], ps.at[at, k], pr.at[at, k], partner
            )
        )

    def pair_sum(reg, half, k):
        ref = pair.at[reg * 2 + half, rows(k)]
        mine = block_terms(reg, halves[half] * 2 + core, k)
        remote(ref, ref, ps.at[reg * 2 + half, k], pr.at[reg * 2 + half, k], partner).wait_recv()
        return mine + pair[reg * 2 + half, rows(k), :].astype(F32)

    def z_out(half, k):
        for d in (0, 1):
            zsend[d * 2 + half, rows(k), :] = pair_sum(1 + d, half, k).astype(BF)
            go(
                remote(
                    zsend.at[d * 2 + half, rows(k)],
                    zgot.at[d * 2 + half, rows(k)],
                    zs.at[d * 2 + half, k],
                    zr.at[d * 2 + half, k],
                    (down, up)[d],
                )
            )

    def region_sum(half, k):
        value = pair_sum(0, half, k)
        for d in (0, 1):
            ref = zgot.at[d * 2 + half, rows(k)]
            remote(ref, ref, zs.at[d * 2 + half, k], zr.at[d * 2 + half, k], up).wait_recv()
            value = value + zgot[d * 2 + half, rows(k), :].astype(F32)
        return value

    def ydev(k):
        return yup if k < 2 else ydown

    def y_out(k):
        ysend[rows(k), :] = region_sum(0, k).astype(BF)
        go(remote(ysend.at[rows(k)], relay.at[rows(k)], ys.at[k], rr.at[k], ydev(k)))

    def relay_on(k):
        ref = relay.at[rows(k)]
        remote(ref, ref, ys.at[k], rr.at[k], yup).wait_recv()
        go(remote(ref, ygot.at[rows(k)], rs.at[k], yr.at[k], ydev(k)))

    def finish(k):
        value = region_sum(1, k) + out_ref[rows(k), :]
        ref = ygot.at[rows(k)]
        remote(ref, ref, rs.at[k], yr.at[k], yup).wait_recv()
        out_ref[rows(k), :] = value + ygot[rows(k), :].astype(F32)

    value = dot3((resid[0], resid[1]), wn, LAST) * inv_ref[...]
    spread[...] = value.astype(BF).reshape(8, BLOCK, 256)

    width = ROWS // planes

    def piece(p):
        return pl.ds(pl.multiple_of(p * width, width), width)

    def plane_copy(p):
        return remote(total.at[piece(p)], plane.at[flat], pls.at[p], plr.at[flat], plane_dev(p))

    for i in (0, 1):
        here = pl.ds(i * 256, 256)
        pair_grad(i).wait_recv()
        total[here, :] = g[core, here, :] + gpair[here, :]

        @pl.loop(i * planes // 2, (i + 1) * planes // 2)
        def _(p):
            @pl.when(p != flat)
            def _():
                plane_copy(p).start()

    run[...] = jnp.zeros((BLOCK, 256), F32)

    @pl.loop(0, 64, unroll=4)
    def _(r):
        at = sel[0, r]
        value = dot(flip_ref[at], spread[at // 8]) + run[...] * sel[1, r].astype(F32)
        run[...] = value
        done[r] = value.astype(BF)

    for k in ORDER:
        pair_out(1, 0, k)
        pair_out(2, 0, k)
    for k in ORDER:
        pair_out(0, 0, k)
    for k in ORDER:
        pair_out(1, 1, k)
        pair_out(2, 1, k)
    for k in ORDER:
        pair_out(0, 1, k)

    plane[flat] = total[piece(flat), :]

    @others
    def _(p):
        remote(plane.at[p], plane.at[p], pls.at[p], plr.at[p], partner).wait_recv()

    summed = plane[0]
    for p in range(1, planes):
        summed = summed + plane[p]
    part[...] = summed.reshape(2, width // 2, 128)
    two_copy = remote(part.at[1 - q], two, qs.at[0], qr.at[0], beside)
    two_copy.start()
    z_out(0, 0)
    two_copy.wait_recv()
    far[h] = part[q] + two[...]

    def far_copy(d):
        return remote(far.at[h], far.at[h], fs.at[d], fr.at[d], me.zto((h + d) % far_n * 2 + q))

    for d in sorted(range(1, far_n), key=lambda d: -min(d, far_n - d)):
        far_copy(d).start()
    for k in ORDER[1:]:
        z_out(0, k)
    out_ref[...] = dot3((resid[0], resid[1]), ws, LAST)
    y_out(0)
    y_out(2)
    for d in range(1, far_n):
        ref = far.at[(h + far_n - d) % far_n]
        remote(ref, ref, fs.at[d], fr.at[d], partner).wait_recv()
    summed = far[0]
    for j in range(1, far_n):
        summed = summed + far[j]
    tile = width // 2

    def inner(j):
        return full.at[core, pl.ds(pl.multiple_of(flat * width + j * tile, tile), tile)]

    full[core, pl.ds(pl.multiple_of(flat * width + q * tile, tile), tile), :] = summed
    again_copy = remote(inner(q), inner(q), aqs.at[0], aqr.at[0], beside)
    again_copy.start()
    for k in ORDER:
        z_out(1, k)
    y_out(1)
    y_out(3)
    remote(inner(1 - q), inner(1 - q), aqs.at[0], aqr.at[0], partner).wait_recv()
    mine = full.at[core, piece(flat)]

    def spread_copy(p):
        return remote(mine, mine, aps.at[p], apr.at[flat], plane_dev(p))

    def last_copy(p):
        ref = full.at[core, piece(p)]
        return remote(ref, ref, gfs.at[p], gfr.at[p], partner)

    @others
    def _(p):
        spread_copy(p).start()

    last_copy(flat).start()
    for k in ORDER:
        relay_on(k)

    @others
    def _(p):
        ref = full.at[core, piece(p)]
        remote(ref, ref, aps.at[p], apr.at[p], partner).wait_recv()
        last_copy(p).start()

    for k in ORDER:
        finish(k)

    @pl.loop(0, planes)
    def _(p):
        ref = full.at[1 - core, piece(p)]
        remote(ref, ref, gfs.at[p], gfr.at[p], partner).wait_recv()

    for i, ref in enumerate((gs_ref, gn_ref)):
        for c in (0, 1):
            ref[:, c * 128 : (c + 1) * 128] = full[c, i * 256 : (i + 1) * 256, :]

    for i in (0, 1):
        pair_grad(i).wait_send()
    two_copy.wait_send()
    again_copy.wait_send()
    for d in range(1, far_n):
        far_copy(d).wait_send()

    @others
    def _(p):
        plane_copy(p).wait_send()
        spread_copy(p).wait_send()

    @pl.loop(0, planes)
    def _(p):
        last_copy(p).wait_send()

    for copy in started:
        copy.wait_send()


def main(nx, nz, block_source, table, wide, flip, inv, base, hot, turned, weights, sel):
    planes, far_n = nx * 4, nz // 2
    width = ROWS // planes
    big = (6, NK)
    return pl.pallas_call(
        functools.partial(main_kernel, nx, nz),
        out_shape=(
            jax.ShapeDtypeStruct((256, 256), F32),
            jax.ShapeDtypeStruct((256, 256), F32),
            jax.ShapeDtypeStruct((ROWS, 256), F32),
        ),
        in_specs=[SM, SM] + [VM] * 8,
        out_specs=(VM,) * 3,
        scratch_shapes=[
            pltpu.VMEM((2, ROWS, 256), BF),
            pltpu.VMEM((2, ROWS, 256), BF),
            pltpu.VMEM((8, BLOCK, 256), BF),
            pltpu.VMEM((BLOCK, 256), F32),
            pltpu.VMEM((64, BLOCK, 256), BF),
            pltpu.VMEM((6, ROWS, 256), BF),
            pltpu.VMEM((2, ROWS, 128), F32),
            pltpu.VMEM((6, ROWS, 256), BF),
            pltpu.VMEM((4, ROWS, 256), BF),
            pltpu.VMEM((4, ROWS, 256), BF),
            pltpu.VMEM((ROWS, 256), BF),
            pltpu.VMEM((ROWS, 256), BF),
            pltpu.VMEM((ROWS, 256), BF),
            pltpu.VMEM((ROWS, 128), F32),
            pltpu.VMEM((ROWS, 128), F32),
            pltpu.VMEM((planes, width, 128), F32),
            pltpu.VMEM((width // 2, 128), F32),
            pltpu.VMEM((far_n, width // 2, 128), F32),
            pltpu.VMEM((2, width // 2, 128), F32),
            pltpu.VMEM((2, ROWS, 128), F32),
            DMA(big), DMA(big), DMA((4, NK)), DMA((4, NK)),
            DMA((NK,)), DMA((NK,)), DMA((NK,)), DMA((NK,)),
            DMA((2,)), DMA((2,)), DMA((planes,)), DMA((planes,)),
            DMA((1,)), DMA((1,)), DMA((far_n,)), DMA((far_n,)),
            DMA((1,)), DMA((1,)), DMA((planes,)), DMA((planes,)),
            DMA((planes,)), DMA((planes,)),
        ],
        compiler_params=pltpu.CompilerParams(
            collective_id=1, has_side_effects=True, vmem_limit_bytes=30 << 20
        ),
        name="main_math",
    )(block_source, sel, table.reshape(96, BLOCK, 256), wide, flip, inv, base, hot, turned, weights)


def store_kernel(a, b, c, a_hbm, b_hbm, c_hbm, sems):
    copies = [
        pltpu.make_async_copy(src, dst, sems.at[i])
        for i, (src, dst) in enumerate(((c, c_hbm), (a, a_hbm), (b, b_hbm)))
    ]
    for copy in copies:
        copy.start()
    for copy in copies:
        copy.wait()


def store(*values):
    return pl.pallas_call(
        store_kernel,
        out_shape=tuple(jax.ShapeDtypeStruct(v.shape, v.dtype) for v in values),
        in_specs=[VM] * 3,
        out_specs=(pl.BlockSpec(memory_space=pltpu.HBM),) * 3,
        scratch_shapes=[DMA((3,))],
        compiler_params=pltpu.CompilerParams(vmem_limit_bytes=8 << 20),
        name="store_results",
    )(*values)


def solution(mesh):
    nx, nz = mesh.shape["row"] // 2, mesh.shape["col"]
    split_rows = P(("row", "col", "rep"))

    def on_device(features, self_weight, neigh_weight, block_source, edge_weights, labels):
        prepared = gather(
            nx, nz, features, self_weight, neigh_weight, block_source, edge_weights, labels
        )
        return store(*main(nx, nz, block_source, *prepared))

    return jax.shard_map(
        on_device,
        mesh=mesh,
        in_specs=(split_rows, P(), P(), split_rows, split_rows, split_rows),
        out_specs=(P(), P(), split_rows),
        check_vma=False,
    )
```

time: 90.8 us -> 67.9 us (0.75)
  Pallas kernels: 84.4 us -> 67 us
  local copies, waits for them, and re-layouts: 5.35 us -> 0.01 us
    pallas_call x3, Pallas kernels: 84.4 us -> 67 us  [the longest x1 37.6 us: main(): pl.pallas_call(functools.partial(main_kernel, nx, nz), out_shape=(jax.Sha...]
    unnamed x18 -> x2, local copies, waits for them, and re-layouts: 4.23 us -> 0.01 us
    slice x1 -> x0, local copies, waits for them, and re-layouts: 1.12 us -> none  [local(): fill = (edge_weights[:, :, 0, 0] > 0).astype(jnp.int32)]
where the time goes in v2:
time: 67.9 us; the launch traced here: 67.7 us
  Pallas kernels  67 us (99%)
    pallas_call x1, Pallas kernels, main(): pl.pallas_call(functools.partial(main_kernel, nx, nz), out_shape=(jax.Sha...  37.6 us
    pallas_call x1, Pallas kernels, gather(): pl.pallas_call(functools.partial(gather_kernel, nx, nz), out_shape=(jax.S...  28.5 us

profile of v2, /device:TPU:1, one launch (start us, length us, event | category | flops | bytes accessed | tf_op | source)
XLA Modules:
  0.0 67.7 jit_solution(7434248397606793322)
XLA Ops:
  0.6 0.0 copy-start
  0.6 28.5 %gather_tables.1 = (bf16[12,512,256]{2,1,0:T(8,128)(2,1)S(1)}, bf16[512,512]{1,0:T(8,128)(2,1)S(1)}, bf16[64,64,64]{2,1,0:T(8,128)(2,1)S(1)}, f32[512,256]{1,0:T...) custom-call(f32[512,256]{1,0:T(8,128)} %f_hbm.1, ...), custom_call_target="tpu_custom_call" | custom-call | tf_op jit(solution)/shard_map/gather_tables/pallas_call | solution.py:247
  29.1 0.0 copy-done
  29.1 37.6 %main_math.1 = (f32[256,256]{1,0:T(8,128)S(1)}, f32[256,256]{1,0:T(8,128)S(1)}, f32[512,256]{1,0:T(8,128)S(1)}) custom-call(s32[8,8]{1,0:T(8,128)S(1)} %copy-done, s32[8,128]{1,0:T(8,128)S(1)} %get-tuple-element.15.sel, bf16[96,64,256]{2,1,0:T(8,128)(2,1)S(1)} %bitcast.2, bf16[512,512]{1,0:T(8,128)(2,1)S(1)} %get-tuple-element.17.wide_ref, ...), custom_call_target="tpu_custom_call" | custom-call | tf_op jit(solution)/shard_map/main_math/pallas_call | solution.py:573
  66.7 1.0 %store_results.1 = (f32[256,256]{1,0:T(8,128)}, f32[256,256]{1,0:T(8,128)}, f32[512,256]{1,0:T(8,128)}) custom-call(f32[256,256]{1,0:T(8,128)S(1)} %get-tuple-element.24.a, f32[256,256]{1,0:T(8,128)S(1)} %get-tuple-element.25.b, f32[512,256]{1,0:T(8,128)S(1)} %get-tuple-element.26.c), custom_call_target="tpu_custom_call" | custom-call | tf_op jit(solution)/shard_map/store_results/pallas_call | solution.py:629
Async XLA Ops:
  0.6 28.5 %copy-start = (s32[8,8]{1,0:T(8,128)S(1)}, s32[8,8]{1,0:T(8,128)}, u32[]{:S(2)}) copy-start(s32[8,8]{1,0:T(8,128)} %src.1) | copy-start | bytes 772

commit v3 on v2

--- a/solution.py
+++ b/solution.py
@@ -16,6 +16,7 @@
 CH = ROWS // NK
 ORDER = (0, 2, 1, 3)
 DMA = pltpu.SemaphoreType.DMA
+REG = pltpu.SemaphoreType.REGULAR
 VM = pl.BlockSpec(memory_space=pltpu.VMEM)
 SM = pl.BlockSpec(memory_space=pltpu.SMEM)
 
@@ -296,7 +297,7 @@
     gs_ref, gn_ref, out_ref,
     mean, resid, spread, run, done, tmsend, g,
     pair, zsend, zgot, ysend, relay, ygot, gpair, total, plane, two, far, part, full,
-    ps, pr, zs, zr, ys, yr, rs, rr, gps, gpr, pls, plr, qs, qr, fs, fr, aqs, aqr, aps, apr, gfs, gfr,
+    ps, pr, zs, zr, ys, yr, rs, rr, gps, gpr, pls, plr, qs, qr, fs, fr, aqs, aqr, aps, apr, gfs, gfr, word, zword,
 ):
     me = Place(nx, nz)
     partner = me.partner()
@@ -312,7 +313,8 @@
     def plane_dev(p):
         return me.at(p // 4, p % 4, z, core)
 
-    barrier = signal((partner, up, down))
+    left, right = me.at((me.x + nx - 1) % nx, me.y, z, core), me.at((me.x + 1) % nx, me.y, z, core)
+    barrier = signal((partner, up, down, yup, ydown, left, right))
 
     def others(body):
         @pl.loop(0, planes)
@@ -321,12 +323,12 @@
             def _():
                 body(p)
 
-    @others
-    def _(p):
-        pl.semaphore_signal(barrier, inc=1, device_id=plane_dev(p), device_id_type=MESH)
-
-    for d in range(1, far_n):
-        pl.semaphore_signal(barrier, inc=1, device_id=me.zto((h + d) % far_n * 2 + q), device_id_type=MESH)
+    def tell(sem, devs):
+        for dev in devs:
+            pl.semaphore_signal(sem, inc=1, device_id=dev, device_id_type=MESH)
+
+    def hear(sem):
+        pl.semaphore_wait(sem, 2)
 
     started = []
 
@@ -357,11 +359,21 @@
         for c in (0, 1):
             g[c, i * 256 : (i + 1) * 256, :] = value[:, c * 128 : (c + 1) * 128]
 
+    pl.semaphore_wait(barrier, 7)
+    tell(word.at[0], (left, right))
+    tell(zword.at[0], (up, down))
     weight_grad(0)
-    pl.semaphore_wait(barrier, 3 + planes - 1 + far_n - 1)
     pair_grad(0).start()
+    hear(word.at[0])
+    tell(word.at[1], (yup, ydown))
+    hear(zword.at[0])
+    tell(zword.at[1], (up, down))
     weight_grad(1)
     pair_grad(1).start()
+    hear(word.at[1])
+    tell(word.at[2], (yup, ydown))
+    hear(zword.at[1])
+    tell(zword.at[2], (up, down))
 
     def block_terms(reg, r, k):
         found = []
@@ -435,16 +447,22 @@
     def plane_copy(p):
         return remote(total.at[piece(p)], plane.at[flat], pls.at[p], plr.at[flat], plane_dev(p))
 
+    hear(zword.at[2])
+    tell(zword.at[3], (up, down))
+    hear(word.at[2])
     for i in (0, 1):
         here = pl.ds(i * 256, 256)
         pair_grad(i).wait_recv()
-        total[here, :] = g[core, here, :] + gpair[here, :]
+        total[here, :] = (g[core, here, :] + gpair[here, :]).astype(BF)
 
         @pl.loop(i * planes // 2, (i + 1) * planes // 2)
         def _(p):
             @pl.when(p != flat)
             def _():
                 plane_copy(p).start()
+
+    hear(zword.at[3])
+    tell(zword.at[4], (up, down))
 
     run[...] = jnp.zeros((BLOCK, 256), F32)
 
@@ -455,6 +473,8 @@
         run[...] = value
         done[r] = value.astype(BF)
 
+    hear(zword.at[4])
+    tell(zword.at[5], (up, down))
     for k in ORDER:
         pair_out(1, 0, k)
         pair_out(2, 0, k)
@@ -465,6 +485,8 @@
         pair_out(2, 1, k)
     for k in ORDER:
         pair_out(0, 1, k)
+    hear(zword.at[5])
+    tell(zword.at[6], (up, down))
 
     plane[flat] = total[piece(flat), :]
 
@@ -472,15 +494,16 @@
     def _(p):
         remote(plane.at[p], plane.at[p], pls.at[p], plr.at[p], partner).wait_recv()
 
-    summed = plane[0]
+    summed = plane[0].astype(F32)
     for p in range(1, planes):
-        summed = summed + plane[p]
+        summed = summed + plane[p].astype(F32)
     part[...] = summed.reshape(2, width // 2, 128)
     two_copy = remote(part.at[1 - q], two, qs.at[0], qr.at[0], beside)
     two_copy.start()
+    hear(zword.at[6])
     z_out(0, 0)
     two_copy.wait_recv()
-    far[h] = part[q] + two[...]
+    far[h] = (part[q] + two[...]).astype(BF)
 
     def far_copy(d):
         return remote(far.at[h], far.at[h], fs.at[d], fr.at[d], me.zto((h + d) % far_n * 2 + q))
@@ -495,15 +518,15 @@
     for d in range(1, far_n):
         ref = far.at[(h + far_n - d) % far_n]
         remote(ref, ref, fs.at[d], fr.at[d], partner).wait_recv()
-    summed = far[0]
+    summed = far[0].astype(F32)
     for j in range(1, far_n):
-        summed = summed + far[j]
+        summed = summed + far[j].astype(F32)
     tile = width // 2
 
     def inner(j):
         return full.at[core, pl.ds(pl.multiple_of(flat * width + j * tile, tile), tile)]
 
-    full[core, pl.ds(pl.multiple_of(flat * width + q * tile, tile), tile), :] = summed
+    full[core, pl.ds(pl.multiple_of(flat * width + q * tile, tile), tile), :] = summed.astype(BF)
     again_copy = remote(inner(q), inner(q), aqs.at[0], aqr.at[0], beside)
     again_copy.start()
     for k in ORDER:
@@ -544,7 +567,7 @@
 
     for i, ref in enumerate((gs_ref, gn_ref)):
         for c in (0, 1):
-            ref[:, c * 128 : (c + 1) * 128] = full[c, i * 256 : (i + 1) * 256, :]
+            ref[:, c * 128 : (c + 1) * 128] = full[c, i * 256 : (i + 1) * 256, :].astype(F32)
 
     for i in (0, 1):
         pair_grad(i).wait_send()
@@ -594,18 +617,19 @@
             pltpu.VMEM((ROWS, 256), BF),
             pltpu.VMEM((ROWS, 256), BF),
             pltpu.VMEM((ROWS, 128), F32),
-            pltpu.VMEM((ROWS, 128), F32),
-            pltpu.VMEM((planes, width, 128), F32),
+            pltpu.VMEM((ROWS, 128), BF),
+            pltpu.VMEM((planes, width, 128), BF),
             pltpu.VMEM((width // 2, 128), F32),
-            pltpu.VMEM((far_n, width // 2, 128), F32),
+            pltpu.VMEM((far_n, width // 2, 128), BF),
             pltpu.VMEM((2, width // 2, 128), F32),
-            pltpu.VMEM((2, ROWS, 128), F32),
+            pltpu.VMEM((2, ROWS, 128), BF),
             DMA(big), DMA(big), DMA((4, NK)), DMA((4, NK)),
             DMA((NK,)), DMA((NK,)), DMA((NK,)), DMA((NK,)),
             DMA((2,)), DMA((2,)), DMA((planes,)), DMA((planes,)),
             DMA((1,)), DMA((1,)), DMA((far_n,)), DMA((far_n,)),
             DMA((1,)), DMA((1,)), DMA((planes,)), DMA((planes,)),
             DMA((planes,)), DMA((planes,)),
+            REG((3,)), REG((7,)),
         ],
         compiler_params=pltpu.CompilerParams(
             collective_id=1, has_side_effects=True, vmem_limit_bytes=30 << 20

time: 67.9 us -> 66.4 us (0.978)
  Pallas kernels: 67 us -> 65.6 us
    pallas_call x1, Pallas kernels: 37.6 us -> 36.2 us  [main(): pl.pallas_call(functools.partial(main_kernel, nx, nz), out_shape=(jax.Sha...]
where the time goes in v3:
time: 66.4 us; the launch traced here: 66.3 us
  Pallas kernels  65.6 us (99%)
    pallas_call x1, Pallas kernels, main(): pl.pallas_call(functools.partial(main_kernel, nx, nz), out_shape=(jax.Sha...  36.2 us
    pallas_call x1, Pallas kernels, gather(): pl.pallas_call(functools.partial(gather_kernel, nx, nz), out_shape=(jax.S...  28.5 us

profile of v3, /device:TPU:1, one launch (start us, length us, event | category | flops | bytes accessed | tf_op | source)
XLA Modules:
  0.0 66.3 jit_solution(13020021229422803598)
XLA Ops:
  0.6 0.0 copy-start
  0.6 28.5 %gather_tables.1 = (bf16[12,512,256]{2,1,0:T(8,128)(2,1)S(1)}, bf16[512,512]{1,0:T(8,128)(2,1)S(1)}, bf16[64,64,64]{2,1,0:T(8,128)(2,1)S(1)}, f32[512,256]{1,0:T...) custom-call(f32[512,256]{1,0:T(8,128)} %f_hbm.1, ...), custom_call_target="tpu_custom_call" | custom-call | tf_op jit(solution)/shard_map/gather_tables/pallas_call | solution.py:248
  29.1 0.0 copy-done
  29.1 36.2 %main_math.1 = (f32[256,256]{1,0:T(8,128)S(1)}, f32[256,256]{1,0:T(8,128)S(1)}, f32[512,256]{1,0:T(8,128)S(1)}) custom-call(s32[8,8]{1,0:T(8,128)S(1)} %copy-done, s32[8,128]{1,0:T(8,128)S(1)} %get-tuple-element.15.sel, bf16[96,64,256]{2,1,0:T(8,128)(2,1)S(1)} %bitcast.2, bf16[512,512]{1,0:T(8,128)(2,1)S(1)} %get-tuple-element.17.wide_ref, ...), custom_call_target="tpu_custom_call" | custom-call | tf_op jit(solution)/shard_map/main_math/pallas_call | solution.py:596
  65.3 1.0 %store_results.1 = (f32[256,256]{1,0:T(8,128)}, f32[256,256]{1,0:T(8,128)}, f32[512,256]{1,0:T(8,128)}) custom-call(f32[256,256]{1,0:T(8,128)S(1)} %get-tuple-element.24.a, f32[256,256]{1,0:T(8,128)S(1)} %get-tuple-element.25.b, f32[512,256]{1,0:T(8,128)S(1)} %get-tuple-element.26.c), custom_call_target="tpu_custom_call" | custom-call | tf_op jit(solution)/shard_map/store_results/pallas_call | solution.py:653
Async XLA Ops:
  0.6 28.5 %copy-start = (s32[8,8]{1,0:T(8,128)S(1)}, s32[8,8]{1,0:T(8,128)}, u32[]{:S(2)}) copy-start(s32[8,8]{1,0:T(8,128)} %src.1) | copy-start | bytes 772

commit v4 on v3

--- a/solution.py
+++ b/solution.py
@@ -16,7 +16,6 @@
 CH = ROWS // NK
 ORDER = (0, 2, 1, 3)
 DMA = pltpu.SemaphoreType.DMA
-REG = pltpu.SemaphoreType.REGULAR
 VM = pl.BlockSpec(memory_space=pltpu.VMEM)
 SM = pl.BlockSpec(memory_space=pltpu.SMEM)
 
@@ -297,7 +296,7 @@
     gs_ref, gn_ref, out_ref,
     mean, resid, spread, run, done, tmsend, g,
     pair, zsend, zgot, ysend, relay, ygot, gpair, total, plane, two, far, part, full,
-    ps, pr, zs, zr, ys, yr, rs, rr, gps, gpr, pls, plr, qs, qr, fs, fr, aqs, aqr, aps, apr, gfs, gfr, word, zword,
+    ps, pr, zs, zr, ys, yr, rs, rr, gps, gpr, pls, plr, qs, qr, fs, fr, aqs, aqr, aps, apr, gfs, gfr, word,
 ):
     me = Place(nx, nz)
     partner = me.partner()
@@ -313,8 +312,16 @@
     def plane_dev(p):
         return me.at(p // 4, p % 4, z, core)
 
-    left, right = me.at((me.x + nx - 1) % nx, me.y, z, core), me.at((me.x + 1) % nx, me.y, z, core)
-    barrier = signal((partner, up, down, yup, ydown, left, right))
+    steps = sorted(
+        ((dx, dy) for dx in range(nx) for dy in range(4) if dx or dy),
+        key=lambda s: -min(s[0], nx - s[0]) - min(s[1], 4 - s[1]),
+    )
+
+    def place(step):
+        return (me.x + step[0]) % nx * 4 + (me.y + step[1]) % 4
+
+    near = [me.zstep(d) for d in (1, nz - 1, 2, nz - 2, 4, nz - 4)]
+    barrier = signal([plane_dev(place(step)) for step in steps] + near + [partner])
 
     def others(body):
         @pl.loop(0, planes)
@@ -322,13 +329,6 @@
             @pl.when(p != flat)
             def _():
                 body(p)
-
-    def tell(sem, devs):
-        for dev in devs:
-            pl.semaphore_signal(sem, inc=1, device_id=dev, device_id_type=MESH)
-
-    def hear(sem):
-        pl.semaphore_wait(sem, 2)
 
     started = []
 
@@ -359,21 +359,13 @@
         for c in (0, 1):
             g[c, i * 256 : (i + 1) * 256, :] = value[:, c * 128 : (c + 1) * 128]
 
-    pl.semaphore_wait(barrier, 7)
-    tell(word.at[0], (left, right))
-    tell(zword.at[0], (up, down))
     weight_grad(0)
+    pl.semaphore_wait(barrier, planes + len(near))
     pair_grad(0).start()
-    hear(word.at[0])
-    tell(word.at[1], (yup, ydown))
-    hear(zword.at[0])
-    tell(zword.at[1], (up, down))
+    for dev in near[4:]:
+        pl.semaphore_signal(word, inc=1, device_id=dev, device_id_type=MESH)
     weight_grad(1)
     pair_grad(1).start()
-    hear(word.at[1])
-    tell(word.at[2], (yup, ydown))
-    hear(zword.at[1])
-    tell(zword.at[2], (up, down))
 
     def block_terms(reg, r, k):
         found = []
@@ -444,25 +436,17 @@
     def piece(p):
         return pl.ds(pl.multiple_of(p * width, width), width)
 
-    def plane_copy(p):
-        return remote(total.at[piece(p)], plane.at[flat], pls.at[p], plr.at[flat], plane_dev(p))
-
-    hear(zword.at[2])
-    tell(zword.at[3], (up, down))
-    hear(word.at[2])
+    def plane_copy(i):
+        p = place(steps[i])
+        return remote(total.at[piece(p)], plane.at[flat], pls.at[i], plr.at[flat], plane_dev(p))
+
     for i in (0, 1):
         here = pl.ds(i * 256, 256)
         pair_grad(i).wait_recv()
         total[here, :] = (g[core, here, :] + gpair[here, :]).astype(BF)
 
-        @pl.loop(i * planes // 2, (i + 1) * planes // 2)
-        def _(p):
-            @pl.when(p != flat)
-            def _():
-                plane_copy(p).start()
-
-    hear(zword.at[3])
-    tell(zword.at[4], (up, down))
+    for i in range(planes - 1):
+        plane_copy(i).start()
 
     run[...] = jnp.zeros((BLOCK, 256), F32)
 
@@ -473,8 +457,6 @@
         run[...] = value
         done[r] = value.astype(BF)
 
-    hear(zword.at[4])
-    tell(zword.at[5], (up, down))
     for k in ORDER:
         pair_out(1, 0, k)
         pair_out(2, 0, k)
@@ -485,8 +467,6 @@
         pair_out(2, 1, k)
     for k in ORDER:
         pair_out(0, 1, k)
-    hear(zword.at[5])
-    tell(zword.at[6], (up, down))
 
     plane[flat] = total[piece(flat), :]
 
@@ -500,7 +480,6 @@
     part[...] = summed.reshape(2, width // 2, 128)
     two_copy = remote(part.at[1 - q], two, qs.at[0], qr.at[0], beside)
     two_copy.start()
-    hear(zword.at[6])
     z_out(0, 0)
     two_copy.wait_recv()
     far[h] = (part[q] + two[...]).astype(BF)
@@ -508,6 +487,7 @@
     def far_copy(d):
         return remote(far.at[h], far.at[h], fs.at[d], fr.at[d], me.zto((h + d) % far_n * 2 + q))
 
+    pl.semaphore_wait(word, 2)
     for d in sorted(range(1, far_n), key=lambda d: -min(d, far_n - d)):
         far_copy(d).start()
     for k in ORDER[1:]:
@@ -536,16 +516,15 @@
     remote(inner(1 - q), inner(1 - q), aqs.at[0], aqr.at[0], partner).wait_recv()
     mine = full.at[core, piece(flat)]
 
-    def spread_copy(p):
-        return remote(mine, mine, aps.at[p], apr.at[flat], plane_dev(p))
+    def spread_copy(i):
+        return remote(mine, mine, aps.at[i], apr.at[flat], plane_dev(place(steps[i])))
 
     def last_copy(p):
         ref = full.at[core, piece(p)]
         return remote(ref, ref, gfs.at[p], gfr.at[p], partner)
 
-    @others
-    def _(p):
-        spread_copy(p).start()
+    for i in range(planes - 1):
+        spread_copy(i).start()
 
     last_copy(flat).start()
     for k in ORDER:
@@ -576,10 +555,9 @@
     for d in range(1, far_n):
         far_copy(d).wait_send()
 
-    @others
-    def _(p):
-        plane_copy(p).wait_send()
-        spread_copy(p).wait_send()
+    for i in range(planes - 1):
+        plane_copy(i).wait_send()
+        spread_copy(i).wait_send()
 
     @pl.loop(0, planes)
     def _(p):
@@ -629,7 +607,7 @@
             DMA((1,)), DMA((1,)), DMA((far_n,)), DMA((far_n,)),
             DMA((1,)), DMA((1,)), DMA((planes,)), DMA((planes,)),
             DMA((planes,)), DMA((planes,)),
-            REG((3,)), REG((7,)),
+            pltpu.SemaphoreType.REGULAR,
         ],
         compiler_params=pltpu.CompilerParams(
             collective_id=1, has_side_effects=True, vmem_limit_bytes=30 << 20

time: 66.4 us -> 63.3 us (0.953)
  Pallas kernels: 65.6 us -> 62.5 us
    pallas_call x1, Pallas kernels: 36.2 us -> 33.1 us  [main(): pl.pallas_call(functools.partial(main_kernel, nx, nz), out_shape=(jax.Sha...]
where the time goes in v4:
time: 63.3 us; the launch traced here: 63.2 us
  Pallas kernels  62.5 us (99%)
  between operations  0.66 us (1%)
    pallas_call x1, Pallas kernels, main(): pl.pallas_call(functools.partial(main_kernel, nx, nz), out_shape=(jax.Sha...  33.1 us
    pallas_call x1, Pallas kernels, gather(): pl.pallas_call(functools.partial(gather_kernel, nx, nz), out_shape=(jax.S...  28.5 us

profile of v4, /device:TPU:1, one launch (start us, length us, event | category | flops | bytes accessed | tf_op | source)
XLA Modules:
  0.0 63.2 jit_solution(14250527088814262499)
XLA Ops:
  0.6 0.0 copy-start
  0.6 28.5 %gather_tables.1 = (bf16[12,512,256]{2,1,0:T(8,128)(2,1)S(1)}, bf16[512,512]{1,0:T(8,128)(2,1)S(1)}, bf16[64,64,64]{2,1,0:T(8,128)(2,1)S(1)}, f32[512,256]{1,0:T...) custom-call(f32[512,256]{1,0:T(8,128)} %f_hbm.1, ...), custom_call_target="tpu_custom_call" | custom-call | tf_op jit(solution)/shard_map/gather_tables/pallas_call | solution.py:247
  29.1 0.0 copy-done
  29.1 33.1 %main_math.1 = (f32[256,256]{1,0:T(8,128)S(1)}, f32[256,256]{1,0:T(8,128)S(1)}, f32[512,256]{1,0:T(8,128)S(1)}) custom-call(s32[8,8]{1,0:T(8,128)S(1)} %copy-done, s32[8,128]{1,0:T(8,128)S(1)} %get-tuple-element.15.sel, bf16[96,64,256]{2,1,0:T(8,128)(2,1)S(1)} %bitcast.2, bf16[512,512]{1,0:T(8,128)(2,1)S(1)} %get-tuple-element.17.wide_ref, ...), custom_call_target="tpu_custom_call" | custom-call | tf_op jit(solution)/shard_map/main_math/pallas_call | solution.py:574
  62.2 1.0 %store_results.1 = (f32[256,256]{1,0:T(8,128)}, f32[256,256]{1,0:T(8,128)}, f32[512,256]{1,0:T(8,128)}) custom-call(f32[256,256]{1,0:T(8,128)S(1)} %get-tuple-element.24.a, f32[256,256]{1,0:T(8,128)S(1)} %get-tuple-element.25.b, f32[512,256]{1,0:T(8,128)S(1)} %get-tuple-element.26.c), custom_call_target="tpu_custom_call" | custom-call | tf_op jit(solution)/shard_map/store_results/pallas_call | solution.py:631
Async XLA Ops:
  0.6 28.5 %copy-start = (s32[8,8]{1,0:T(8,128)S(1)}, s32[8,8]{1,0:T(8,128)}, u32[]{:S(2)}) copy-start(s32[8,8]{1,0:T(8,128)} %src.1) | copy-start | bytes 772

commit v5 on v4

--- a/solution.py
+++ b/solution.py
@@ -296,7 +296,7 @@
     gs_ref, gn_ref, out_ref,
     mean, resid, spread, run, done, tmsend, g,
     pair, zsend, zgot, ysend, relay, ygot, gpair, total, plane, two, far, part, full,
-    ps, pr, zs, zr, ys, yr, rs, rr, gps, gpr, pls, plr, qs, qr, fs, fr, aqs, aqr, aps, apr, gfs, gfr, word,
+    ps, pr, zs, zr, ys, yr, rs, rr, gps, gpr, pls, plr, qs, qr, fs, fr, aps, apr, gfs, gfr, word,
 ):
     me = Place(nx, nz)
     partner = me.partner()
@@ -305,7 +305,6 @@
     yup, ydown = me.ystep(1), me.ystep(3)
     flat = me.x * 4 + me.y
     q, h = z % 2, z // 2
-    far_n = nz // 2
     planes = nx * 4
     beside = me.zto(2 * h + 1 - q)
 
@@ -320,7 +319,7 @@
     def place(step):
         return (me.x + step[0]) % nx * 4 + (me.y + step[1]) % 4
 
-    near = [me.zstep(d) for d in (1, nz - 1, 2, nz - 2, 4, nz - 4)]
+    near = [me.zstep(d) for d in (1, nz - 1, 2, nz - 2, 3, nz - 3, 4, nz - 4)]
     barrier = signal([plane_dev(place(step)) for step in steps] + near + [partner])
 
     def others(body):
@@ -362,7 +361,7 @@
     weight_grad(0)
     pl.semaphore_wait(barrier, planes + len(near))
     pair_grad(0).start()
-    for dev in near[4:]:
+    for dev in near[6:]:
         pl.semaphore_signal(word, inc=1, device_id=dev, device_id_type=MESH)
     weight_grad(1)
     pair_grad(1).start()
@@ -428,9 +427,6 @@
         remote(ref, ref, rs.at[k], yr.at[k], yup).wait_recv()
         out_ref[rows(k), :] = value + ygot[rows(k), :].astype(F32)
 
-    value = dot3((resid[0], resid[1]), wn, LAST) * inv_ref[...]
-    spread[...] = value.astype(BF).reshape(8, BLOCK, 256)
-
     width = ROWS // planes
 
     def piece(p):
@@ -440,13 +436,20 @@
         p = place(steps[i])
         return remote(total.at[piece(p)], plane.at[flat], pls.at[i], plr.at[flat], plane_dev(p))
 
-    for i in (0, 1):
+    def plane_out(i):
         here = pl.ds(i * 256, 256)
         pair_grad(i).wait_recv()
         total[here, :] = (g[core, here, :] + gpair[here, :]).astype(BF)
-
-    for i in range(planes - 1):
-        plane_copy(i).start()
+        for j in range(planes - 1):
+
+            @pl.when(place(steps[j]) * 2 // planes == i)
+            def _():
+                plane_copy(j).start()
+
+    plane_out(0)
+    value = dot3((resid[0], resid[1]), wn, LAST) * inv_ref[...]
+    spread[...] = value.astype(BF).reshape(8, BLOCK, 256)
+    plane_out(1)
 
     run[...] = jnp.zeros((BLOCK, 256), F32)
 
@@ -482,51 +485,45 @@
     two_copy.start()
     z_out(0, 0)
     two_copy.wait_recv()
-    far[h] = (part[q] + two[...]).astype(BF)
+    far[z] = (part[q] + two[...]).astype(BF)
 
     def far_copy(d):
-        return remote(far.at[h], far.at[h], fs.at[d], fr.at[d], me.zto((h + d) % far_n * 2 + q))
+        return remote(far.at[z], far.at[z], fs.at[d], fr.at[d], me.zstep(d))
 
     pl.semaphore_wait(word, 2)
-    for d in sorted(range(1, far_n), key=lambda d: -min(d, far_n - d)):
+    for d in sorted(range(1, nz), key=lambda d: -min(d, nz - d)):
         far_copy(d).start()
     for k in ORDER[1:]:
         z_out(0, k)
     out_ref[...] = dot3((resid[0], resid[1]), ws, LAST)
     y_out(0)
     y_out(2)
-    for d in range(1, far_n):
-        ref = far.at[(h + far_n - d) % far_n]
+    for d in range(1, nz):
+        ref = far.at[(z + nz - d) % nz]
         remote(ref, ref, fs.at[d], fr.at[d], partner).wait_recv()
-    summed = far[0].astype(F32)
-    for j in range(1, far_n):
-        summed = summed + far[j].astype(F32)
     tile = width // 2
-
-    def inner(j):
-        return full.at[core, pl.ds(pl.multiple_of(flat * width + j * tile, tile), tile)]
-
-    full[core, pl.ds(pl.multiple_of(flat * width + q * tile, tile), tile), :] = summed.astype(BF)
-    again_copy = remote(inner(q), inner(q), aqs.at[0], aqr.at[0], beside)
-    again_copy.start()
+    for j in (0, 1):
+        summed = far[j].astype(F32)
+        for i in range(j + 2, nz, 2):
+            summed = summed + far[i].astype(F32)
+        here = pl.ds(pl.multiple_of(flat * width + j * tile, tile), tile)
+        full[core, here, :] = summed.astype(BF)
+    mine = full.at[core, piece(flat)]
+
+    def spread_copy(i):
+        return remote(mine, mine, aps.at[i], apr.at[flat], plane_dev(place(steps[i])))
+
+    def last_copy(p):
+        ref = full.at[core, piece(p)]
+        return remote(ref, ref, gfs.at[p], gfr.at[p], partner)
+
+    for i in range(planes - 1):
+        spread_copy(i).start()
+    last_copy(flat).start()
     for k in ORDER:
         z_out(1, k)
     y_out(1)
     y_out(3)
-    remote(inner(1 - q), inner(1 - q), aqs.at[0], aqr.at[0], partner).wait_recv()
-    mine = full.at[core, piece(flat)]
-
-    def spread_copy(i):
-        return remote(mine, mine, aps.at[i], apr.at[flat], plane_dev(place(steps[i])))
-
-    def last_copy(p):
-        ref = full.at[core, piece(p)]
-        return remote(ref, ref, gfs.at[p], gfr.at[p], partner)
-
-    for i in range(planes - 1):
-        spread_copy(i).start()
-
-    last_copy(flat).start()
     for k in ORDER:
         relay_on(k)
 
@@ -551,8 +548,7 @@
     for i in (0, 1):
         pair_grad(i).wait_send()
     two_copy.wait_send()
-    again_copy.wait_send()
-    for d in range(1, far_n):
+    for d in range(1, nz):
         far_copy(d).wait_send()
 
     for i in range(planes - 1):
@@ -568,7 +564,7 @@
 
 
 def main(nx, nz, block_source, table, wide, flip, inv, base, hot, turned, weights, sel):
-    planes, far_n = nx * 4, nz // 2
+    planes = nx * 4
     width = ROWS // planes
     big = (6, NK)
     return pl.pallas_call(
@@ -598,14 +594,14 @@
             pltpu.VMEM((ROWS, 128), BF),
             pltpu.VMEM((planes, width, 128), BF),
             pltpu.VMEM((width // 2, 128), F32),
-            pltpu.VMEM((far_n, width // 2, 128), BF),
+            pltpu.VMEM((nz, width // 2, 128), BF),
             pltpu.VMEM((2, width // 2, 128), F32),
             pltpu.VMEM((2, ROWS, 128), BF),
             DMA(big), DMA(big), DMA((4, NK)), DMA((4, NK)),
             DMA((NK,)), DMA((NK,)), DMA((NK,)), DMA((NK,)),
             DMA((2,)), DMA((2,)), DMA((planes,)), DMA((planes,)),
-            DMA((1,)), DMA((1,)), DMA((far_n,)), DMA((far_n,)),
-            DMA((1,)), DMA((1,)), DMA((planes,)), DMA((planes,)),
+            DMA((1,)), DMA((1,)), DMA((nz,)), DMA((nz,)),
+            DMA((planes,)), DMA((planes,)),
             DMA((planes,)), DMA((planes,)),
             pltpu.SemaphoreType.REGULAR,
         ],

time: 63.3 us -> 62.2 us (0.983)
  Pallas kernels: 62.5 us -> 60.8 us
    pallas_call x1, Pallas kernels: 33.1 us -> 31.4 us  [main(): pl.pallas_call(functools.partial(main_kernel, nx, nz), out_shape=(jax.Sha...]
where the time goes in v5:
time: 62.2 us; the launch traced here: 61.5 us
  Pallas kernels  60.8 us (98%)
  between operations  0.66 us (1%)
    pallas_call x1, Pallas kernels, main(): pl.pallas_call(functools.partial(main_kernel, nx, nz), out_shape=(jax.Sha...  31.4 us
    pallas_call x1, Pallas kernels, gather(): pl.pallas_call(functools.partial(gather_kernel, nx, nz), out_shape=(jax.S...  28.5 us

profile of v5, /device:TPU:1, one launch (start us, length us, event | category | flops | bytes accessed | tf_op | source)
XLA Modules:
  0.0 61.5 jit_solution(6221034851811533914)
XLA Ops:
  0.6 0.0 copy-start
  0.6 28.5 %gather_tables.1 = (bf16[12,512,256]{2,1,0:T(8,128)(2,1)S(1)}, bf16[512,512]{1,0:T(8,128)(2,1)S(1)}, bf16[64,64,64]{2,1,0:T(8,128)(2,1)S(1)}, f32[512,256]{1,0:T...) custom-call(f32[512,256]{1,0:T(8,128)} %f_hbm.1, ...), custom_call_target="tpu_custom_call" | custom-call | tf_op jit(solution)/shard_map/gather_tables/pallas_call | solution.py:247
  29.1 0.0 copy-done
  29.1 31.4 %main_math.1 = (f32[256,256]{1,0:T(8,128)S(1)}, f32[256,256]{1,0:T(8,128)S(1)}, f32[512,256]{1,0:T(8,128)S(1)}) custom-call(s32[8,8]{1,0:T(8,128)S(1)} %copy-done, s32[8,128]{1,0:T(8,128)S(1)} %get-tuple-element.15.sel, bf16[96,64,256]{2,1,0:T(8,128)(2,1)S(1)} %bitcast.2, bf16[512,512]{1,0:T(8,128)(2,1)S(1)} %get-tuple-element.17.wide_ref, ...), custom_call_target="tpu_custom_call" | custom-call | tf_op jit(solution)/shard_map/main_math/pallas_call | solution.py:570
  60.5 1.0 %store_results.1 = (f32[256,256]{1,0:T(8,128)}, f32[256,256]{1,0:T(8,128)}, f32[512,256]{1,0:T(8,128)}) custom-call(f32[256,256]{1,0:T(8,128)S(1)} %get-tuple-element.24.a, f32[256,256]{1,0:T(8,128)S(1)} %get-tuple-element.25.b, f32[512,256]{1,0:T(8,128)S(1)} %get-tuple-element.26.c), custom_call_target="tpu_custom_call" | custom-call | tf_op jit(solution)/shard_map/store_results/pallas_call | solution.py:627
Async XLA Ops:
  0.6 28.5 %copy-start = (s32[8,8]{1,0:T(8,128)S(1)}, s32[8,8]{1,0:T(8,128)}, u32[]{:S(2)}) copy-start(s32[8,8]{1,0:T(8,128)} %src.1) | copy-start | bytes 772

commit v6 on v5

--- a/solution.py
+++ b/solution.py
@@ -483,7 +483,7 @@
     part[...] = summed.reshape(2, width // 2, 128)
     two_copy = remote(part.at[1 - q], two, qs.at[0], qr.at[0], beside)
     two_copy.start()
-    z_out(0, 0)
+    out_ref[...] = dot3((resid[0], resid[1]), ws, LAST)
     two_copy.wait_recv()
     far[z] = (part[q] + two[...]).astype(BF)
 
@@ -493,9 +493,8 @@
     pl.semaphore_wait(word, 2)
     for d in sorted(range(1, nz), key=lambda d: -min(d, nz - d)):
         far_copy(d).start()
-    for k in ORDER[1:]:
+    for k in ORDER:
         z_out(0, k)
-    out_ref[...] = dot3((resid[0], resid[1]), ws, LAST)
     y_out(0)
     y_out(2)
     for d in range(1, nz):

time: 62.2 us -> 63.2 us (1.016)
  the two profiles are of different devices: /device:TPU:1 before, /device:TPU:8 now
where the time goes in v6:
time: 63.2 us; the launch traced here: 63.1 us
  Pallas kernels  62.4 us (99%)
  between operations  0.66 us (1%)
    pallas_call x1, Pallas kernels, main(): pl.pallas_call(functools.partial(main_kernel, nx, nz), out_shape=(jax.Sha...  35.1 us
    pallas_call x1, Pallas kernels, gather(): pl.pallas_call(functools.partial(gather_kernel, nx, nz), out_shape=(jax.S...  26.3 us

profile of v6, /device:TPU:8, one launch (start us, length us, event | category | flops | bytes accessed | tf_op | source)
XLA Modules:
  0.0 63.1 jit_solution(2797477453970553511)
XLA Ops:
  0.6 0.0 copy-start
  0.6 26.3 %gather_tables.1 = (bf16[12,512,256]{2,1,0:T(8,128)(2,1)S(1)}, bf16[512,512]{1,0:T(8,128)(2,1)S(1)}, bf16[64,64,64]{2,1,0:T(8,128)(2,1)S(1)}, f32[512,256]{1,0:T...) custom-call(f32[512,256]{1,0:T(8,128)} %f_hbm.1, ...), custom_call_target="tpu_custom_call" | custom-call | tf_op jit(solution)/shard_map/gather_tables/pallas_call | solution.py:247
  27.0 0.0 copy-done
  27.0 35.1 %main_math.1 = (f32[256,256]{1,0:T(8,128)S(1)}, f32[256,256]{1,0:T(8,128)S(1)}, f32[512,256]{1,0:T(8,128)S(1)}) custom-call(s32[8,8]{1,0:T(8,128)S(1)} %copy-done, s32[8,128]{1,0:T(8,128)S(1)} %get-tuple-element.15.sel, bf16[96,64,256]{2,1,0:T(8,128)(2,1)S(1)} %bitcast.2, bf16[512,512]{1,0:T(8,128)(2,1)S(1)} %get-tuple-element.17.wide_ref, ...), custom_call_target="tpu_custom_call" | custom-call | tf_op jit(solution)/shard_map/main_math/pallas_call | solution.py:569
  62.1 1.0 %store_results.1 = (f32[256,256]{1,0:T(8,128)}, f32[256,256]{1,0:T(8,128)}, f32[512,256]{1,0:T(8,128)}) custom-call(f32[256,256]{1,0:T(8,128)S(1)} %get-tuple-element.24.a, f32[256,256]{1,0:T(8,128)S(1)} %get-tuple-element.25.b, f32[512,256]{1,0:T(8,128)S(1)} %get-tuple-element.26.c), custom_call_target="tpu_custom_call" | custom-call | tf_op jit(solution)/shard_map/store_results/pallas_call | solution.py:626
Async XLA Ops:
  0.6 26.4 %copy-start = (s32[8,8]{1,0:T(8,128)S(1)}, s32[8,8]{1,0:T(8,128)}, u32[]{:S(2)}) copy-start(s32[8,8]{1,0:T(8,128)} %src.1) | copy-start | bytes 772
